TPU v7x, 128 devices: a whole 4x4x4 slice. The times are simulated.
128 devices in a mesh: leaf: 4 (over x), front: 32 (over z, y, core).
Axes of the slice: x: 4, y: 4, z: 4, core: 2. Of those that a mesh axis runs over, the one named last changes fastest.
Arguments:
- probe_seeds: int32 [32], replicated, may hold values from 0 to 32748
- leaf_inverse: bfloat16 [4, 4096, 4096], P('leaf', 'front'), as said below
- leaf_update: bfloat16 [4, 4096, 16384], P('leaf', 'front'), may hold values from -0.046875 to 0.046875
- internal_inverse: bfloat16 [4, 4096, 4096], P('leaf', 'front'), as said below
- internal_update: bfloat16 [4, 4096, 16384], P('leaf', 'front'), may hold values from -0.046875 to 0.046875
- child_map: int32 [4, 2, 256], P('leaf'), may hold values from 0 to 320, as said below
Outputs:
- leaf_solution: float32 [4, 32, 4096], P('leaf', None, 'front')
- internal_solution: float32 [4, 32, 4096], P('leaf', None, 'front')
Inputs may be any that keep to these rules, and one draw needn't show every extreme that they name: `child_map`: in each row of a slot and child the entries other than 320 are distinct; the last row is not read. `leaf_inverse`: each supernode's matrix is lower triangular with a positive diagonal. `internal_inverse`: each slot's matrix is lower triangular with a positive diagonal.
All inputs are finite; a program needn't handle non-finite values.
Results may differ from a plain program's by a relative error of at most 0.0065.
Values may be sent and summed in bfloat16 or wider, within the bound.
A program may use at most 64 MiB of HBM per device.

v0:
```python
import functools

import jax
import jax.numpy as jnp
from jax import lax
from jax.experimental import pallas as pl
from jax.experimental.pallas import tpu as pltpu
from jax.sharding import PartitionSpec as P

BLOCK = 64
MOD = 32749
MESH = pl.DeviceIdType.MESH
NT = (((1,), (1,)), ((), ()))


def mod_prime(x):
    q = (x.astype(jnp.float32) * (1.0 / MOD)).astype(jnp.int32)
    r = x - q * MOD
    r = jnp.where(r < 0, r + MOD, r)
    return jnp.where(r >= MOD, r - MOD, r)


def probe_signs(seeds, node_id, columns, start, shape):
    index = node_id * columns + start + lax.broadcasted_iota(jnp.int32, shape, 1)
    wrapped = index >= MOD
    lower = jnp.where(wrapped, index - MOD, index)
    upper = jnp.where(wrapped, 1, 0)
    hashed = mod_prime(lower * 30011 + upper * 7717 + seeds)
    hashed = mod_prime(hashed * hashed)
    hashed = mod_prime(hashed * 21143 + lower)
    hashed = mod_prime(hashed * hashed + upper)
    return (1 - 2 * ((hashed >> 3) & 1)).astype(jnp.float32)


def kernel(
    fronts,
    probes,
    columns,
    width,
    seeds_ref,
    maps_ref,
    leaf_inv_hbm,
    leaf_upd_hbm,
    inner_inv_hbm,
    inner_upd_hbm,
    leaf_out,
    inner_out,
    leaf_inv,
    leaf_upd,
    inner_inv,
    inner_upd,
    to_slot,
    to_root,
    slot_root,
    signs,
    all_maps,
    table_v,
    table_s,
    send_part,
    recv_part,
    own_chunk,
    recv_all,
    hop_send,
    hop_up,
    hop_root,
    hop_chunk,
    leaf_y,
    leaf_v,
    load_sem,
    table_sem,
    map_send,
    map_recv,
    part_send,
    part_recv,
    all_send,
    all_recv,
    hop_send_sem,
    hop_up_sem,
    hop_root_sem,
    hop_chunk_sem,
):
    x = lax.axis_index("leaf")
    m = lax.axis_index("front")
    leaves = 4
    f32, bf16 = jnp.float32, jnp.bfloat16
    is_slot = (x == 0) | (x == 2)
    is_root = x == 1

    loads = [
        pltpu.make_async_copy(src.at[0], dst, load_sem.at[i])
        for i, (src, dst) in enumerate(
            (
                (leaf_inv_hbm, leaf_inv),
                (leaf_upd_hbm, leaf_upd),
                (inner_upd_hbm, inner_upd),
                (inner_inv_hbm, inner_inv),
            )
        )
    ]
    for load in loads:
        load.start()

    barrier = pltpu.get_barrier_semaphore()

    def greet_front(i, carry):
        pl.semaphore_signal(
            barrier, inc=1, device_id=(x, lax.rem(m + i, fronts)), device_id_type=MESH
        )
        return carry

    lax.fori_loop(1, fronts, greet_front, 0)
    for i in range(1, leaves):
        pl.semaphore_signal(
            barrier, inc=1, device_id=(lax.rem(x + i, leaves), m), device_id_type=MESH
        )

    seeds = jnp.zeros((probes, 1), jnp.int32)
    row = lax.broadcasted_iota(jnp.int32, (probes, 1), 0)
    for p in range(probes):
        seeds = jnp.where(row == p, seeds_ref[p], seeds)

    piece = 512

    def make_signs(i, carry):
        start = pl.multiple_of(i * piece, piece)
        z = probe_signs(seeds, x, columns, start, (probes, piece))
        signs[:, pl.ds(start, piece)] = z.astype(bf16)
        return carry

    lax.fori_loop(0, columns // piece, make_signs, 0)
    own_signs = probe_signs(seeds, x + 1 + leaves, columns, m * width, (probes, width))

    pl.semaphore_wait(barrier, fronts - 1 + leaves - 1)

    map_copies = []
    for i in range(1, leaves):
        copy = pltpu.make_async_remote_copy(
            src_ref=maps_ref.at[0],
            dst_ref=all_maps.at[x],
            send_sem=map_send.at[i - 1],
            recv_sem=map_recv.at[i - 1],
            device_id=(lax.rem(x + i, leaves), m),
            device_id_type=MESH,
        )
        copy.start()
        map_copies.append(copy)
    all_maps[x] = maps_ref[0]

    def rows_times(vector, matrix):
        return lax.dot_general(vector, matrix, NT, preferred_element_type=f32)

    loads[0].wait()
    y_leaf = rows_times(signs[...], leaf_inv[...])
    leaf_y[...] = y_leaf

    for copy in map_copies:
        copy.wait()

    blocks = columns // BLOCK
    count = all_maps.shape[2]
    slot_pair = all_maps[pl.ds((x // 2) * 2, 1)][0]
    slot_map = jnp.where(x % 2 == 0, slot_pair[0:1], slot_pair[1:2])
    root_pair = all_maps[1]
    root_map = jnp.where(x // 2 == 0, root_pair[0:1], root_pair[1:2])
    target = lax.broadcasted_iota(jnp.int32, (blocks, count), 0)
    source = lax.broadcasted_iota(jnp.int32, (blocks, count), 1) + 1

    def find(values, wanted):
        return jnp.max(jnp.where(values == wanted, source, 0), axis=1, keepdims=True)

    direct = find(slot_map, target)
    inner = find(root_map, target)
    through = find(slot_map, jnp.where(inner == 0, -1, inner + (blocks - 1)))
    lane = lax.broadcasted_iota(jnp.int32, (blocks, 128), 1)
    sub = lax.broadcasted_iota(jnp.int32, (blocks, 128), 0)

    def as_row(column):
        return jnp.sum(jnp.where(lane == sub, column, 0), axis=0, keepdims=True)

    table_v[...] = jnp.zeros((8, 128), jnp.int32)
    table_v[0:1, :] = as_row(direct)
    table_v[1:2, :] = as_row(through)
    table_v[2:3, :] = as_row(inner)
    table_copy = pltpu.make_async_copy(table_v, table_s, table_sem)
    table_copy.start()
    table_copy.wait()

    def pick_columns(matrix, table, out):
        left_half = lax.broadcasted_iota(jnp.int32, (width, 128), 1) < BLOCK

        def half(entry, side):
            block = jnp.maximum(entry - 1, 0)
            at = (block >> 1) * 128
            tile = matrix[:, pl.ds(at, 128)].astype(f32)
            turned = pltpu.roll(tile, BLOCK, 1)
            odd = jnp.full((width, 128), block & 1, jnp.int32)
            found = jnp.full((width, 128), entry, jnp.int32)
            here = jnp.where(odd == side, tile, turned)
            return jnp.where(found > 0, here, 0.0)

        def body(j, carry):
            first = half(table_s[table, 2 * j], 0)
            second = half(table_s[table, 2 * j + 1], 1)
            at = pl.multiple_of(j * 128, 128)
            out[:, pl.ds(at, 128)] = jnp.where(left_half, first, second).astype(bf16)
            return carry

        lax.fori_loop(0, blocks // 2, body, 0, unroll=2)

    def sum_start(which, vector, matrix, more=None):
        partial = jnp.dot(vector, matrix[...], preferred_element_type=f32)
        if more is not None:
            partial = partial + more
        for j in range(fronts):
            send_part[which, j] = partial[:, j * width : (j + 1) * width].astype(bf16)
        recv_part[which, m] = send_part[which, m]

        def send(i, carry):
            j = lax.rem(m + i, fronts)
            pltpu.make_async_remote_copy(
                src_ref=send_part.at[which, j],
                dst_ref=recv_part.at[which, m],
                send_sem=part_send.at[which],
                recv_sem=part_recv.at[which],
                device_id=(x, j),
                device_id_type=MESH,
            ).start()
            return carry

        lax.fori_loop(1, fronts, send, 0)

    def wait_for(buffer, sem):
        part = buffer.at[pl.ds(0, fronts - 1)]
        pltpu.make_async_copy(part, part, sem).wait()

    def sum_finish(which):
        wait_for(recv_part.at[which], part_recv.at[which])
        total = recv_part[which, 0].astype(f32)
        for j in range(1, fronts):
            total = total + recv_part[which, j].astype(f32)
        return total

    def share_start(which, chunk_ref):
        def send(i, carry):
            j = lax.rem(m + i, fronts)
            pltpu.make_async_remote_copy(
                src_ref=chunk_ref,
                dst_ref=recv_all.at[which, m],
                send_sem=all_send.at[which],
                recv_sem=all_recv.at[which],
                device_id=(x, j),
                device_id_type=MESH,
            ).start()
            return carry

        lax.fori_loop(1, fronts, send, 0)
        recv_all[which, m] = chunk_ref[...]

    def share_finish(which):
        wait_for(recv_all.at[which], all_recv.at[which])
        return jnp.concatenate([recv_all[which, j] for j in range(fronts)], axis=1)

    def hop(src, dst, send_sem, recv_sem, to):
        return pltpu.make_async_remote_copy(
            src_ref=src,
            dst_ref=dst,
            send_sem=send_sem,
            recv_sem=recv_sem,
            device_id=(to, m),
            device_id_type=MESH,
        )

    LEAF_SUM, ROOT_SUM, BACK_SUM, LAST_SUM = 0, 1, 2, 3
    RESIDUAL, ROOT_X, SLOT_X = 0, 1, 2

    yb_leaf = y_leaf.astype(bf16)
    loads[1].wait()
    pick_columns(leaf_upd, 0, to_slot)
    sum_start(LEAF_SUM, yb_leaf, to_slot)
    pick_columns(leaf_upd, 1, to_root)

    hop_up_copy = hop(hop_send.at[0], hop_up, hop_send_sem.at[0], hop_up_sem, jnp.maximum(x - 1, 0))
    root_copy = hop(hop_send.at[1], hop_root.at[x], hop_send_sem.at[1], hop_root_sem.at[x], 1)

    def send_to_root():
        hop_send[1] = sum_finish(ROOT_SUM)
        root_copy.start()

    @pl.when(jnp.logical_not(is_slot))
    def _():
        hop_send[0] = sum_finish(LEAF_SUM)
        hop_up_copy.start()
        sum_start(ROOT_SUM, yb_leaf, to_root)
        loads[2].wait()
        loads[3].wait()

    @pl.when(is_slot)
    def _():
        own_sum = sum_finish(LEAF_SUM)
        hop_up_copy.wait_recv()
        own_chunk[RESIDUAL] = (own_signs - (own_sum + hop_up[...])).astype(bf16)
        share_start(RESIDUAL, own_chunk.at[RESIDUAL])
        loads[2].wait()
        pick_columns(inner_upd, 2, slot_root)
        carried = jnp.dot(yb_leaf, to_root[...], preferred_element_type=f32)
        loads[3].wait()
        y_slot = rows_times(share_finish(RESIDUAL), inner_inv[...])
        sum_start(ROOT_SUM, y_slot.astype(bf16), slot_root, carried)
        leaf_v[...] = y_slot
        send_to_root()

    @pl.when(x == 3)
    def _():
        send_to_root()

    @pl.when(is_root)
    def _():
        total = sum_finish(ROOT_SUM)
        for other in (0, 2, 3):
            hop(hop_send.at[1], hop_root.at[other], hop_send_sem.at[1], hop_root_sem.at[other], 1).wait_recv()
            total = total + hop_root[other]
        own_chunk[RESIDUAL] = (own_signs - total).astype(bf16)
        share_start(RESIDUAL, own_chunk.at[RESIDUAL])
        y_root = rows_times(share_finish(RESIDUAL), inner_inv[...])
        sum_start(BACK_SUM, y_root.astype(bf16), inner_inv)
        result = sum_finish(BACK_SUM)
        own_chunk[ROOT_X] = result.astype(bf16)
        for i, other in enumerate((0, 2, 3)):
            hop(own_chunk.at[ROOT_X], hop_chunk.at[0], hop_send_sem.at[2 + i], hop_chunk_sem.at[0], other).start()
        share_start(ROOT_X, own_chunk.at[ROOT_X])
        inner_out[0] = result

    @pl.when(jnp.logical_not(is_root))
    def _():
        hop(own_chunk.at[ROOT_X], hop_chunk.at[0], hop_send_sem.at[2], hop_chunk_sem.at[0], 1).wait_recv()
        share_start(ROOT_X, hop_chunk.at[0])

    x_root = share_finish(ROOT_X)

    @pl.when(is_slot)
    def _():
        v = rows_times(x_root, slot_root[...])
        s = (leaf_v[...] - v).astype(bf16)
        sum_start(BACK_SUM, s, inner_inv)

    leaf_v[...] = rows_times(x_root, to_root[...])

    @pl.when(is_slot)
    def _():
        result = sum_finish(BACK_SUM)
        own_chunk[SLOT_X] = result.astype(bf16)
        hop(own_chunk.at[SLOT_X], hop_chunk.at[1], hop_send_sem.at[2], hop_chunk_sem.at[1], x + 1).start()
        share_start(SLOT_X, own_chunk.at[SLOT_X])
        inner_out[0] = result

    @pl.when(jnp.logical_not(is_slot))
    def _():
        hop(own_chunk.at[SLOT_X], hop_chunk.at[1], hop_send_sem.at[5], hop_chunk_sem.at[1], x - 1).wait_recv()
        share_start(SLOT_X, hop_chunk.at[1])

    @pl.when(x == 3)
    def _():
        inner_out[0] = jnp.zeros((probes, width), f32)

    x_slot = share_finish(SLOT_X)
    v = rows_times(x_slot, to_slot[...]) + leaf_v[...]
    s = (leaf_y[...] - v).astype(bf16)
    sum_start(LAST_SUM, s, leaf_inv)
    leaf_out[0] = sum_finish(LAST_SUM)

    for which in (LEAF_SUM, ROOT_SUM, LAST_SUM):
        wait_for(send_part.at[which], part_send.at[which])
    for which in (ROOT_X, SLOT_X):
        wait_for(recv_all.at[which], all_send.at[which])

    @pl.when(x != 3)
    def _():
        wait_for(send_part.at[BACK_SUM], part_send.at[BACK_SUM])
        wait_for(recv_all.at[RESIDUAL], all_send.at[RESIDUAL])

    @pl.when(jnp.logical_not(is_slot))
    def _():
        hop_up_copy.wait_send()

    @pl.when(jnp.logical_not(is_root))
    def _():
        root_copy.wait_send()

    @pl.when(is_slot)
    def _():
        hop(own_chunk.at[SLOT_X], hop_chunk.at[1], hop_send_sem.at[2], hop_chunk_sem.at[1], x + 1).wait_send()

    @pl.when(is_root)
    def _():
        for i, other in enumerate((0, 2, 3)):
            hop(own_chunk.at[ROOT_X], hop_chunk.at[0], hop_send_sem.at[2 + i], hop_chunk_sem.at[0], other).wait_send()


def shards(probe_seeds, leaf_inverse, leaf_update, internal_inverse, internal_update, child_map):
    fronts = lax.axis_size("front")
    leaves = lax.axis_size("leaf")
    probes = probe_seeds.shape[0]
    width, columns = leaf_inverse.shape[1:]
    rows = leaf_update.shape[2]
    f32, bf16 = jnp.float32, jnp.bfloat16
    dma = pltpu.SemaphoreType.DMA
    vmem = pl.BlockSpec(memory_space=pltpu.VMEM)
    hbm = pl.BlockSpec(memory_space=pl.ANY)
    out = jax.ShapeDtypeStruct((1, probes, width), f32)
    return pl.pallas_call(
        functools.partial(kernel, fronts, probes, columns, width),
        out_shape=(out, out),
        in_specs=[pl.BlockSpec(memory_space=pltpu.SMEM), vmem, hbm, hbm, hbm, hbm],
        out_specs=(vmem, vmem),
        scratch_shapes=[
            pltpu.VMEM((width, columns), bf16),
            pltpu.VMEM((width, rows), bf16),
            pltpu.VMEM((width, columns), bf16),
            pltpu.VMEM((width, rows), bf16),
            pltpu.VMEM((width, columns), bf16),
            pltpu.VMEM((width, columns), bf16),
            pltpu.VMEM((width, columns), bf16),
            pltpu.VMEM((probes, columns), bf16),
            pltpu.VMEM((leaves, *child_map.shape[1:]), jnp.int32),
            pltpu.VMEM((8, 128), jnp.int32),
            pltpu.SMEM((8, 128), jnp.int32),
            pltpu.VMEM((4, fronts, probes, width), bf16),
            pltpu.VMEM((4, fronts, probes, width), bf16),
            pltpu.VMEM((3, probes, width), bf16),
            pltpu.VMEM((3, fronts, probes, width), bf16),
            pltpu.VMEM((2, probes, width), f32),
            pltpu.VMEM((probes, width), f32),
            pltpu.VMEM((leaves, probes, width), f32),
            pltpu.VMEM((2, probes, width), bf16),
            pltpu.VMEM((probes, width), f32),
            pltpu.VMEM((probes, width), f32),
            dma((4,)),
            dma,
            dma((3,)),
            dma((3,)),
            dma((4,)),
            dma((4,)),
            dma((3,)),
            dma((3,)),
            dma((6,)),
            dma,
            dma((4,)),
            dma((2,)),
        ],
        compiler_params=pltpu.CompilerParams(
            collective_id=0, has_side_effects=True, vmem_limit_bytes=40 * 1024 * 1024
        ),
        name="solves",
    )(probe_seeds, child_map, leaf_inverse, leaf_update, internal_inverse, internal_update)


def solution(mesh):
    return jax.shard_map(
        shards,
        mesh=mesh,
        in_specs=(
            P(),
            P("leaf", "front", None),
            P("leaf", "front", None),
            P("leaf", "front", None),
            P("leaf", "front", None),
            P("leaf", None, None),
        ),
        out_specs=(P("leaf", None, "front"), P("leaf", None, "front")),
        check_vma=False,
    )
```

profile of v0, /device:TPU:3, one launch (start us, length us, event | category | flops | bytes accessed | tf_op | source)
XLA Modules:
  0.0 90.5 jit_solution(3197551585039424656)
XLA Ops:
  0.6 0.0 copy-start
  0.6 2.2 %copy-done = bf16[1,128,16384]{2,1,0:T(8,128)(2,1)S(1)} copy-done((bf16[1,128,16384]{2,1,0:T(8,128)(2,1)S(1)}, bf16[1,128,16384]{2,1,0:T(8,128)(2,1)}, u32[]{:S(2)}) %copy-start) | copy-done | bytes 4194328
  2.8 0.0 copy-start.1
  2.8 2.2 %copy-done.1 = bf16[1,128,16384]{2,1,0:T(8,128)(2,1)S(1)} copy-done((bf16[1,128,16384]{2,1,0:T(8,128)(2,1)S(1)}, bf16[1,128,16384]{2,1,0:T(8,128)(2,1)}, u32[]{:S(2)}) %copy-start.1) | copy-done | bytes 4194328
  5.0 0.0 copy-start.2
  5.0 1.2 %copy-done.2 = bf16[1,128,4096]{2,1,0:T(8,128)(2,1)S(1)} copy-done((bf16[1,128,4096]{2,1,0:T(8,128)(2,1)S(1)}, bf16[1,128,4096]{2,1,0:T(8,128)(2,1)}, u32[]{:S(2)}) %copy-start.2) | copy-done | bytes 1048600
  6.2 0.0 copy-start.3
  6.2 1.2 %copy-done.3 = bf16[1,128,4096]{2,1,0:T(8,128)(2,1)S(1)} copy-done((bf16[1,128,4096]{2,1,0:T(8,128)(2,1)S(1)}, bf16[1,128,4096]{2,1,0:T(8,128)(2,1)}, u32[]{:S(2)}) %copy-start.3) | copy-done | bytes 1048600
  7.5 0.0 copy-start.4
  7.5 0.7 copy-done.4
  8.1 0.0 copy-start.5
  8.1 0.7 copy-done.5
  8.8 80.5 %solves.1 = (f32[1,32,128]{2,1,0:T(8,128)S(1)}, f32[1,32,128]{2,1,0:T(8,128)S(1)}) custom-call(s32[32]{0:T(128)S(1)} %copy-done.5, s32[1,2,256]{2,1,0:T(2,128)S(1)} %copy-done.4, bf16[1,128,4096]{2,1,0:T(8,128)(2,1)S(1)} %copy-done.2, bf16[1,128,16384]{2,1,0:T(8,128)(2,1)S(1)} %copy-done, bf16[1,128,4096]{2,1,0:T(8,128)(2,1)S(1)} %copy-done.3, ...), custom_call_target="tpu_custom_call" | custom-call | tf_op jit(solution)/shard_map/solves/pallas_call | solution.py:410
  89.3 0.6 copy.10
  89.9 0.6 copy.11
Async XLA Ops:
  0.6 2.2 %copy-start = (bf16[1,128,16384]{2,1,0:T(8,128)(2,1)S(1)}, bf16[1,128,16384]{2,1,0:T(8,128)(2,1)}, u32[]{:S(2)}) copy-start(bf16[1,128,16384]{2,1,0:T(8,128)(2,1)} %leaf_upd_hbm.1) | copy-start | bytes 12582916
  2.8 2.2 %copy-start.1 = (bf16[1,128,16384]{2,1,0:T(8,128)(2,1)S(1)}, bf16[1,128,16384]{2,1,0:T(8,128)(2,1)}, u32[]{:S(2)}) copy-start(bf16[1,128,16384]{2,1,0:T(8,128)(2,1)} %inner_upd_hbm.1) | copy-start | bytes 12582916
  5.0 1.2 %copy-start.2 = (bf16[1,128,4096]{2,1,0:T(8,128)(2,1)S(1)}, bf16[1,128,4096]{2,1,0:T(8,128)(2,1)}, u32[]{:S(2)}) copy-start(bf16[1,128,4096]{2,1,0:T(8,128)(2,1)} %leaf_inv_hbm.1) | copy-start | bytes 3145732
  6.2 1.2 %copy-start.3 = (bf16[1,128,4096]{2,1,0:T(8,128)(2,1)S(1)}, bf16[1,128,4096]{2,1,0:T(8,128)(2,1)}, u32[]{:S(2)}) copy-start(bf16[1,128,4096]{2,1,0:T(8,128)(2,1)} %inner_inv_hbm.1) | copy-start | bytes 3145732
  7.5 0.7 copy-start.4
  8.1 0.7 copy-start.5
where the time goes:
time: 90.8 us; the launch traced here: 90.5 us
  Pallas kernels  80.5 us (89%)
  local copies, waits for them, and re-layouts  9.37 us (10%)
    pallas_call x1, Pallas kernels, shards(): pl.pallas_call(functools.partial(kernel, fronts, probes, columns, width),...  80.5 us
    unnamed x14, local copies, waits for them, and re-layouts  9.37 us

commit v1 on v0

v1 whole, which is shorter than its diff:
```python
import functools

import jax
import jax.numpy as jnp
from jax import lax
from jax.experimental import pallas as pl
from jax.experimental.pallas import tpu as pltpu
from jax.sharding import PartitionSpec as P

BLOCK = 64
MOD = 32749
MESH = pl.DeviceIdType.MESH
NT = (((1,), (1,)), ((), ()))
OFFSETS = (
    (2, 2), (2, 1), (1, 2), (2, 3), (3, 2), (2, 0), (0, 2), (1, 1),
    (3, 3), (1, 3), (3, 1), (1, 0), (0, 1), (3, 0), (0, 3), (0, 0),
)


def packed(values):
    word = sum(v << (2 * i) for i, v in enumerate(values))
    return word - (1 << 32) if word >= 1 << 31 else word


OFFSET_Z = packed([z for z, _ in OFFSETS])
OFFSET_Y = packed([y for _, y in OFFSETS])


def mod_prime(x):
    q = (x.astype(jnp.float32) * (1.0 / MOD)).astype(jnp.int32)
    r = x - q * MOD
    r = jnp.where(r < 0, r + MOD, r)
    return jnp.where(r >= MOD, r - MOD, r)


def probe_signs(seeds, node_id, columns, start, shape):
    index = node_id * columns + start + lax.broadcasted_iota(jnp.int32, shape, 1)
    wrapped = index >= MOD
    lower = jnp.where(wrapped, index - MOD, index)
    upper = jnp.where(wrapped, 1, 0)
    hashed = mod_prime(lower * 30011 + upper * 7717 + seeds)
    hashed = mod_prime(hashed * hashed)
    hashed = mod_prime(hashed * 21143 + lower)
    hashed = mod_prime(hashed * hashed + upper)
    return (1 - 2 * ((hashed >> 3) & 1)).astype(jnp.float32)


def kernel(
    fronts,
    probes,
    columns,
    width,
    seeds_hbm,
    maps_hbm,
    leaf_inv_hbm,
    leaf_upd_hbm,
    inner_inv_hbm,
    inner_upd_hbm,
    leaf_hbm,
    inner_hbm,
    seeds_s,
    leaf_inv,
    leaf_upd,
    inner_inv,
    inner_upd,
    to_slot,
    to_root,
    slot_root,
    root_inv,
    signs,
    leaf_all,
    carried,
    all_maps,
    table_v,
    table_s,
    send_part,
    recv_part,
    own_chunk,
    recv_all,
    hop_send,
    hop_up,
    hop_root,
    hop_root_x,
    hop_slot_x,
    leaf_y,
    inner_y,
    leaf_v,
    leaf_out,
    inner_out,
    load_sem,
    small_sem,
    map_send,
    map_recv,
    part_send,
    part_recv,
    all_send,
    all_recv,
    hop_up_send,
    hop_up_recv,
    hop_root_send,
    hop_root_recv,
    hop_x_send,
    hop_x_recv,
    bulk_send,
    bulk_recv,
    out_sem,
):
    x = lax.axis_index("leaf")
    m = lax.axis_index("front")
    m_z, m_y, m_c = m // 8, lax.rem(m // 2, 4), lax.rem(m, 2)
    leaves = 4
    f32, bf16 = jnp.float32, jnp.bfloat16
    is_slot = (x == 0) | (x == 2)
    is_root = x == 1
    part_rows = probes // 2
    halves = (0, 1)

    def rows_of(h):
        return pl.ds(h * part_rows, part_rows)

    seed_copy = pltpu.make_async_copy(seeds_hbm, seeds_s, small_sem.at[0])
    map_copy = pltpu.make_async_copy(maps_hbm.at[0], all_maps.at[x], small_sem.at[1])
    seed_copy.start()
    map_copy.start()
    loads = [
        pltpu.make_async_copy(src.at[0], dst, load_sem.at[i])
        for i, (src, dst) in enumerate(
            (
                (leaf_inv_hbm, leaf_inv),
                (leaf_upd_hbm, leaf_upd),
                (inner_upd_hbm, inner_upd),
                (inner_inv_hbm, inner_inv),
            )
        )
    ]
    loads[0].start()
    loads[1].start()

    def peer(i):
        at = (i // 2) * 2
        z = lax.rem(m_z + ((jnp.int32(OFFSET_Z) >> at) & 3), 4)
        y = lax.rem(m_y + ((jnp.int32(OFFSET_Y) >> at) & 3), 4)
        return z * 8 + y * 2 + lax.rem(m_c + 1 + i, 2)

    barrier = pltpu.get_barrier_semaphore()

    def greet_front(i, carry):
        pl.semaphore_signal(barrier, inc=1, device_id=(x, peer(i)), device_id_type=MESH)
        return carry

    lax.fori_loop(0, fronts - 1, greet_front, 0)
    for i in range(1, leaves):
        pl.semaphore_signal(
            barrier, inc=1, device_id=(lax.rem(x + i, leaves), m), device_id_type=MESH
        )

    ROOT_AT = 1

    def map_to(to, kind):
        return pltpu.make_async_remote_copy(
            src_ref=maps_hbm.at[0],
            dst_ref=all_maps.at[x],
            send_sem=map_send.at[to],
            recv_sem=map_recv.at[kind],
            device_id=(to, m),
            device_id_type=MESH,
        )

    def slot_map_copy(to):
        return pltpu.make_async_remote_copy(
            src_ref=maps_hbm.at[0],
            dst_ref=all_maps.at[x],
            send_sem=map_send.at[0],
            recv_sem=map_recv.at[0],
            device_id=(to, m),
            device_id_type=MESH,
        )

    bulk_rows = width // 4

    def bulk_copy(piece, to):
        rows = pl.ds(piece * bulk_rows, bulk_rows)
        return pltpu.make_async_remote_copy(
            src_ref=inner_inv_hbm.at[0, rows],
            dst_ref=root_inv.at[rows],
            send_sem=bulk_send.at[to // 2],
            recv_sem=bulk_recv,
            device_id=(to, m),
            device_id_type=MESH,
        )

    greeted = fronts - 1 + leaves - 1

    @pl.when(is_slot)
    def _():
        pl.semaphore_wait(barrier, greeted)
        slot_map_copy(x + 1).start()

    seed_copy.wait()
    seeds = jnp.zeros((probes, 1), jnp.int32)
    row = lax.broadcasted_iota(jnp.int32, (probes, 1), 0)
    for p in range(probes):
        seeds = jnp.where(row == p, seeds_s[p], seeds)

    piece = 512

    def make_signs(i, carry):
        start = pl.multiple_of(i * piece, piece)
        z = probe_signs(seeds, x, columns, start, (probes, piece))
        signs[:, pl.ds(start, piece)] = z.astype(bf16)
        return carry

    lax.fori_loop(0, columns // piece, make_signs, 0)

    def rows_times(vector, matrix):
        return lax.dot_general(vector, matrix[...], NT, preferred_element_type=f32)

    loads[0].wait()
    leaf_y[...] = rows_times(signs[...], leaf_inv)
    yb_leaf = leaf_y[...].astype(bf16)
    loads[1].wait()
    loads[2].start()
    loads[3].start()
    wide = 2048

    def leaf_products(i, carry):
        at = pl.ds(pl.multiple_of(i * wide, wide), wide)
        leaf_all[:, at] = jnp.dot(
            yb_leaf, leaf_upd[:, at], preferred_element_type=f32
        ).astype(bf16)
        return carry

    lax.fori_loop(0, leaf_upd.shape[1] // wide, leaf_products, 0)
    map_copy.wait()

    @pl.when(jnp.logical_not(is_slot))
    def _():
        pl.semaphore_wait(barrier, greeted)

    @pl.when(is_root)
    def _():
        for to in (0, 2, 3):
            map_to(to, 1).start()
        bulk_copy(0, 0).start()
        for q in range(4):
            bulk_copy(q, 2).start()

    blocks = columns // BLOCK
    count = all_maps.shape[2]
    target = lax.broadcasted_iota(jnp.int32, (blocks, count), 0)
    source = lax.broadcasted_iota(jnp.int32, (blocks, count), 1) + 1
    lane = lax.broadcasted_iota(jnp.int32, (blocks, 128), 1)
    sub = lax.broadcasted_iota(jnp.int32, (blocks, 128), 0)

    def find(values, wanted):
        return jnp.max(jnp.where(values == wanted, source, 0), axis=1, keepdims=True)

    def as_row(column):
        return jnp.sum(jnp.where(lane == sub, column, 0), axis=0, keepdims=True)

    def slot_map():
        pair = all_maps[pl.ds((x // 2) * 2, 1)][0]
        return jnp.where(x % 2 == 0, pair[0:1], pair[1:2])

    def table_out(which):
        copy = pltpu.make_async_copy(table_v.at[which], table_s.at[which], small_sem.at[2])
        copy.start()
        copy.wait()

    table_v[...] = jnp.zeros(table_v.shape, jnp.int32)

    @pl.when(jnp.logical_not(is_slot))
    def _():
        slot_map_copy(x).wait_recv()

    table_v[0, 0:1, :] = as_row(find(slot_map(), target))
    table_out(0)

    def pick(read, table, at, rows, write):
        left_half = lax.broadcasted_iota(jnp.int32, (rows, 128), 1) < BLOCK

        def half(entry, side):
            block = jnp.maximum(entry - 1, 0)
            odd = jnp.full((rows, 128), block & 1, jnp.int32)
            found = jnp.full((rows, 128), entry, jnp.int32)
            tile = read((block >> 1) * 128).astype(f32)
            turned = pltpu.roll(tile, BLOCK, 1)
            here = jnp.where(odd == side, tile, turned)
            return jnp.where(found > 0, here, 0.0)

        def body(j, carry):
            first = half(table_s[table, at, 2 * j], 0)
            second = half(table_s[table, at, 2 * j + 1], 1)
            write(j, jnp.where(left_half, first, second).astype(bf16))
            return carry

        lax.fori_loop(0, blocks // 2, body, 0, unroll=4)

    def pick_matrix(matrix, table, at, out):
        def write(j, tile):
            out[:, pl.ds(pl.multiple_of(j * 128, 128), 128)] = tile

        pick(lambda start: matrix[:, pl.ds(start, 128)], table, at, width, write)

    def pick_products(table, at, write):
        pick(lambda start: leaf_all[:, pl.ds(start, 128)], table, at, probes, write)

    def to_peers(src, dst, send_sem, recv_sem):
        def send(i, carry):
            j = peer(i)
            pltpu.make_async_remote_copy(
                src_ref=src(j),
                dst_ref=dst,
                send_sem=send_sem,
                recv_sem=recv_sem,
                device_id=(x, j),
                device_id_type=MESH,
            ).start()
            return carry

        lax.fori_loop(0, fronts - 1, send, 0)

    def wait_for(buffer, sem):
        part = buffer.at[pl.ds(0, fronts - 1)]
        pltpu.make_async_copy(part, part, sem).wait()

    def parts_start(which, h):
        to_peers(
            lambda j: send_part.at[which, h, j],
            recv_part.at[which, h, m],
            part_send.at[which, h],
            part_recv.at[which, h],
        )
        recv_part[which, h, m] = send_part[which, h, m]

    def sum_start(which, h, vector, matrix, more=None):
        partial = jnp.dot(vector, matrix[...], preferred_element_type=f32)
        for j in range(fronts):
            chunk = partial[:, j * width : (j + 1) * width]
            if more is not None:
                chunk = chunk + more[h, j].astype(f32)
            send_part[which, h, j] = chunk.astype(bf16)
        parts_start(which, h)

    def sum_finish(which, h):
        wait_for(recv_part.at[which, h], part_recv.at[which, h])
        sums = []
        for q in range(4):
            total = recv_part[which, h, q].astype(f32)
            for j in range(q + 4, fronts, 4):
                total = total + recv_part[which, h, j].astype(f32)
            sums.append(total)
        return (sums[0] + sums[1]) + (sums[2] + sums[3])

    def share_start(which, h, chunk_ref):
        to_peers(
            lambda j: chunk_ref,
            recv_all.at[which, h, m],
            all_send.at[which, h],
            all_recv.at[which, h],
        )
        recv_all[which, h, m] = chunk_ref[...]

    def share_finish(which, h):
        wait_for(recv_all.at[which, h], all_recv.at[which, h])
        return jnp.concatenate([recv_all[which, h, j] for j in range(fronts)], axis=1)

    def hop(src, dst, send_sem, recv_sem, to):
        return pltpu.make_async_remote_copy(
            src_ref=src,
            dst_ref=dst,
            send_sem=send_sem,
            recv_sem=recv_sem,
            device_id=(to, m),
            device_id_type=MESH,
        )

    LEAF_SUM, ROOT_SUM, ROOT_BACK, SLOT_BACK, LAST_SUM = 0, 1, 2, 3, 4
    SLOT_RHS, ROOT_RHS, ROOT_X, SLOT_X = 0, 1, 2, 3

    def up_copy(h, to):
        return hop(hop_send.at[0, h], hop_up.at[h], hop_up_send.at[h], hop_up_recv.at[h], to)

    def root_copy(h, i, origin, to):
        return hop(
            hop_root.at[origin, h], hop_root.at[origin, h], hop_root_send.at[i, h], hop_root_recv.at[origin, h], to
        )

    def root_x_copy(h, to):
        return hop(hop_send.at[1, h], hop_root_x.at[h], hop_x_send.at[0, h], hop_x_recv.at[0, h], to)

    def slot_x_copy(h, to):
        return hop(own_chunk.at[SLOT_X, h], hop_slot_x.at[h], hop_x_send.at[1, h], hop_x_recv.at[1, h], to)

    def half_of(value, h):
        return value[h * part_rows : (h + 1) * part_rows]

    def write_leaf_part(j, tile):
        for h in halves:
            send_part[LEAF_SUM, h, j] = tile[h * part_rows : (h + 1) * part_rows]

    pick_products(0, 0, write_leaf_part)
    for h in halves:
        parts_start(LEAF_SUM, h)

    @pl.when(jnp.logical_not(is_root))
    def _():
        map_to(0, 1).wait_recv()

    root_pair = all_maps[1]
    root_map = jnp.where(x // 2 == 0, root_pair[0:1], root_pair[1:2])
    inner = find(root_map, target)
    through = find(slot_map(), jnp.where(inner == 0, -1, inner + (blocks - 1)))
    table_v[1, 0:1, :] = as_row(through)
    table_v[1, 1:2, :] = as_row(inner)
    table_out(1)

    @pl.when(jnp.logical_not(is_slot))
    def _():
        for h in halves:
            hop_send[0, h] = sum_finish(LEAF_SUM, h)
            up_copy(h, x - 1).start()

        @pl.when(is_root)
        def _():
            for q in range(1, 4):
                bulk_copy(q, 0).start()

        def write_root_part(j, tile):
            for h in halves:
                send_part[ROOT_SUM, h, j] = half_of(tile, h)

        pick_products(1, 0, write_root_part)
        for h in halves:
            parts_start(ROOT_SUM, h)
        loads[2].wait()
        loads[3].wait()
        pick_matrix(leaf_upd, 0, 0, to_slot)
        pick_matrix(leaf_upd, 1, 0, to_root)
        for h in halves:
            hop_root[x, h] = sum_finish(ROOT_SUM, h)
            for i, to in enumerate((0, 2)):
                root_copy(h, i, x, to).start()

    @pl.when(is_slot)
    def _():
        def write_carried(j, tile):
            for h in halves:
                carried[h, j] = half_of(tile, h)

        pick_products(1, 0, write_carried)
        loads[2].wait()
        pick_matrix(inner_upd, 1, 1, slot_root)
        slot_signs = probe_signs(seeds, x + 1 + leaves, columns, m * width, (probes, width))
        root_signs = probe_signs(seeds, ROOT_AT + 1 + leaves, columns, m * width, (probes, width))
        loads[3].wait()
        for h in halves:
            own_sum = sum_finish(LEAF_SUM, h)
            up_copy(h, x).wait_recv()
            own_chunk[SLOT_RHS, h] = (half_of(slot_signs, h) - (own_sum + hop_up[h])).astype(bf16)
            share_start(SLOT_RHS, h, own_chunk.at[SLOT_RHS, h])
        pick_matrix(leaf_upd, 0, 0, to_slot)
        for h in halves:
            y_slot = rows_times(share_finish(SLOT_RHS, h), inner_inv)
            inner_y[rows_of(h)] = y_slot
            sum_start(ROOT_SUM, h, y_slot.astype(bf16), slot_root, carried)
        pick_matrix(leaf_upd, 1, 0, to_root)
        for h in halves:
            hop_root[x, h] = sum_finish(ROOT_SUM, h)
            root_copy(h, 0, x, 2 - x).start()
        for h in halves:
            for origin in (1, 3):
                root_copy(h, 0, origin, x).wait_recv()
            root_copy(h, 0, 2 - x, x).wait_recv()
            total = (hop_root[0, h] + hop_root[1, h]) + (hop_root[2, h] + hop_root[3, h])
            own_chunk[ROOT_RHS, h] = (half_of(root_signs, h) - total).astype(bf16)
            share_start(ROOT_RHS, h, own_chunk.at[ROOT_RHS, h])
        pltpu.make_async_copy(root_inv, root_inv, bulk_recv).wait()
        for h in halves:
            y_root = rows_times(share_finish(ROOT_RHS, h), root_inv)
            sum_start(ROOT_BACK, h, y_root.astype(bf16), root_inv)
        for h in halves:
            result = sum_finish(ROOT_BACK, h)
            own_chunk[ROOT_X, h] = result.astype(bf16)
            hop_send[1, h] = result
            root_x_copy(h, x + 1).start()
            share_start(ROOT_X, h, own_chunk.at[ROOT_X, h])
        for h in halves:
            x_root = share_finish(ROOT_X, h)
            s = (inner_y[rows_of(h)] - rows_times(x_root, slot_root)).astype(bf16)
            sum_start(SLOT_BACK, h, s, inner_inv)
        for h in halves:
            x_root = jnp.concatenate([recv_all[ROOT_X, h, j] for j in range(fronts)], axis=1)
            leaf_v[rows_of(h)] = leaf_y[rows_of(h)] - rows_times(x_root, to_root)
        for h in halves:
            result = sum_finish(SLOT_BACK, h)
            own_chunk[SLOT_X, h] = result.astype(bf16)
            slot_x_copy(h, x + 1).start()
            share_start(SLOT_X, h, own_chunk.at[SLOT_X, h])
            inner_out[rows_of(h)] = result

    @pl.when(jnp.logical_not(is_slot))
    def _():
        for h in halves:
            root_x_copy(h, x).wait_recv()
            own_chunk[ROOT_X, h] = hop_root_x[h].astype(bf16)
            share_start(ROOT_X, h, own_chunk.at[ROOT_X, h])
            inner_out[rows_of(h)] = jnp.where(is_root, hop_root_x[h], 0.0)
        for h in halves:
            x_root = share_finish(ROOT_X, h)
            leaf_v[rows_of(h)] = leaf_y[rows_of(h)] - rows_times(x_root, to_root)
        for h in halves:
            slot_x_copy(h, x).wait_recv()
            share_start(SLOT_X, h, hop_slot_x.at[h])

    for h in halves:
        x_slot = share_finish(SLOT_X, h)
        s = (leaf_v[rows_of(h)] - rows_times(x_slot, to_slot)).astype(bf16)
        sum_start(LAST_SUM, h, s, leaf_inv)
    inner_write = pltpu.make_async_copy(inner_out, inner_hbm.at[0], out_sem.at[2])
    inner_write.start()
    leaf_writes = [
        pltpu.make_async_copy(leaf_out.at[rows_of(h)], leaf_hbm.at[0, rows_of(h)], out_sem.at[h])
        for h in halves
    ]
    for h in halves:
        leaf_out[rows_of(h)] = sum_finish(LAST_SUM, h)
        leaf_writes[h].start()

    for h in halves:
        for which in (LEAF_SUM, ROOT_SUM, LAST_SUM):
            wait_for(send_part.at[which, h], part_send.at[which, h])
        for which in (ROOT_X, SLOT_X):
            wait_for(recv_all.at[which, h], all_send.at[which, h])

    @pl.when(is_slot)
    def _():
        slot_map_copy(x + 1).wait_send()
        for h in halves:
            for which in (ROOT_BACK, SLOT_BACK):
                wait_for(send_part.at[which, h], part_send.at[which, h])
            for which in (SLOT_RHS, ROOT_RHS):
                wait_for(recv_all.at[which, h], all_send.at[which, h])
            root_copy(h, 0, x, 2 - x).wait_send()
            root_x_copy(h, x + 1).wait_send()
            slot_x_copy(h, x + 1).wait_send()

    @pl.when(jnp.logical_not(is_slot))
    def _():
        for h in halves:
            up_copy(h, x - 1).wait_send()
            for i, to in enumerate((0, 2)):
                root_copy(h, i, x, to).wait_send()

    @pl.when(is_root)
    def _():
        for to in (0, 2, 3):
            map_to(to, 1).wait_send()
        for to in (0, 2):
            pltpu.make_async_copy(root_inv, root_inv, bulk_send.at[to // 2]).wait()

    inner_write.wait()
    for copy in leaf_writes:
        copy.wait()


def write_out(leaf_ref, inner_ref, leaf_hbm, inner_hbm, sem):
    copies = [
        pltpu.make_async_copy(leaf_ref, leaf_hbm, sem.at[0]),
        pltpu.make_async_copy(inner_ref, inner_hbm, sem.at[1]),
    ]
    for copy in copies:
        copy.start()
    for copy in copies:
        copy.wait()


def shards(probe_seeds, leaf_inverse, leaf_update, internal_inverse, internal_update, child_map):
    fronts = lax.axis_size("front")
    leaves = lax.axis_size("leaf")
    probes = probe_seeds.shape[0]
    width, columns = leaf_inverse.shape[1:]
    rows = leaf_update.shape[2]
    f32, bf16 = jnp.float32, jnp.bfloat16
    dma = pltpu.SemaphoreType.DMA
    hbm = pl.BlockSpec(memory_space=pltpu.HBM)
    out = jax.ShapeDtypeStruct((1, probes, width), f32)
    part = (probes // 2, width)
    leaf_part, inner_part = pl.pallas_call(
        functools.partial(kernel, fronts, probes, columns, width),
        out_shape=(out, out),
        in_specs=[hbm] * 6,
        out_specs=(hbm, hbm),
        scratch_shapes=[
            pltpu.SMEM((probes,), jnp.int32),
            pltpu.VMEM((width, columns), bf16),
            pltpu.VMEM((width, rows), bf16),
            pltpu.VMEM((width, columns), bf16),
            pltpu.VMEM((width, rows), bf16),
            pltpu.VMEM((width, columns), bf16),
            pltpu.VMEM((width, columns), bf16),
            pltpu.VMEM((width, columns), bf16),
            pltpu.VMEM((width, columns), bf16),
            pltpu.VMEM((probes, columns), bf16),
            pltpu.VMEM((probes, rows), bf16),
            pltpu.VMEM((2, fronts, *part), bf16),
            pltpu.VMEM((leaves, *child_map.shape[1:]), jnp.int32),
            pltpu.VMEM((2, 8, 128), jnp.int32),
            pltpu.SMEM((2, 8, 128), jnp.int32),
            pltpu.VMEM((5, 2, fronts, *part), bf16),
            pltpu.VMEM((5, 2, fronts, *part), bf16),
            pltpu.VMEM((4, 2, *part), bf16),
            pltpu.VMEM((4, 2, fronts, *part), bf16),
            pltpu.VMEM((2, 2, *part), f32),
            pltpu.VMEM((2, *part), f32),
            pltpu.VMEM((leaves, 2, *part), f32),
            pltpu.VMEM((2, *part), f32),
            pltpu.VMEM((2, *part), bf16),
            pltpu.VMEM((probes, width), f32),
            pltpu.VMEM((probes, width), f32),
            pltpu.VMEM((probes, width), f32),
            pltpu.VMEM((probes, width), f32),
            pltpu.VMEM((probes, width), f32),
            dma((4,)),
            dma((3,)),
            dma((leaves,)),
            dma((2,)),
            dma((5, 2)),
            dma((5, 2)),
            dma((4, 2)),
            dma((4, 2)),
            dma((2,)),
            dma((2,)),
            dma((2, 2)),
            dma((leaves, 2)),
            dma((2, 2)),
            dma((2, 2)),
            dma((2,)),
            dma,
            dma((3,)),
        ],
        compiler_params=pltpu.CompilerParams(
            collective_id=0, has_side_effects=True, vmem_limit_bytes=60 * 1024 * 1024
        ),
        name="solves",
    )(probe_seeds, child_map, leaf_inverse, leaf_update, internal_inverse, internal_update)
    return pl.pallas_call(
        write_out,
        out_shape=(out, out),
        in_specs=[hbm, hbm],
        out_specs=(hbm, hbm),
        scratch_shapes=[dma((2,))],
        name="write_out",
    )(leaf_part, inner_part)


def solution(mesh):
    return jax.shard_map(
        shards,
        mesh=mesh,
        in_specs=(
            P(),
            P("leaf", "front", None),
            P("leaf", "front", None),
            P("leaf", "front", None),
            P("leaf", "front", None),
            P("leaf", None, None),
        ),
        out_specs=(P("leaf", None, "front"), P("leaf", None, "front")),
        check_vma=False,
    )
```

time: 90.8 us -> 77.4 us (0.85)
  local copies, waits for them, and re-layouts: 9.37 us -> 0 us
  Pallas kernels: 80.5 us -> 76.7 us
    unnamed x14 -> x0, local copies, waits for them, and re-layouts: 9.37 us -> none
    pallas_call x1, Pallas kernels: 80.5 us -> 74.6 us  [shards(): pl.pallas_call(functools.partial(kernel, fronts, probes, columns, width),...]
    pallas_call x0 -> x1, Pallas kernels: none -> 2.11 us  [shards(): pl.pallas_call(write_out, out_shape=(out, out), in_specs=[hbm, hbm], out_...]
where the time goes in v1:
time: 77.4 us; the launch traced here: 77.3 us
  Pallas kernels  76.7 us (99%)
    pallas_call x1, Pallas kernels, shards(): pl.pallas_call(functools.partial(kernel, fronts, probes, columns, width),...  74.6 us
    pallas_call x1, Pallas kernels, shards(): pl.pallas_call(write_out, out_shape=(out, out), in_specs=[hbm, hbm], out_...  2.11 us

profile of v1, /device:TPU:3, one launch (start us, length us, event | category | flops | bytes accessed | tf_op | source)
XLA Modules:
  0.0 77.3 jit_solution(5640993971466834421)
XLA Ops:
  0.6 74.6 %solves.1 = (f32[1,32,128]{2,1,0:T(8,128)}, f32[1,32,128]{2,1,0:T(8,128)}) custom-call(s32[32]{0:T(128)} %seeds_hbm.1, s32[1,2,256]{2,1,0:T(2,128)} %maps_hbm.1, bf16[1,128,4096]{2,1,0:T(8,128)(2,1)} %leaf_inv_hbm.1, bf16[1,128,16384]{2,1,0:T(8,128)(2,1)} %leaf_upd_hbm.1, bf16[1,128,4096]{2,1,0:T(8,128)(2,1)} %inner_inv_hbm.1, ...), custom_call_target="tpu_custom_call" | custom-call | tf_op jit(solution)/shard_map/solves/pallas_call | solution.py:589
  75.2 2.1 %write_out.1 = (f32[1,32,128]{2,1,0:T(8,128)}, f32[1,32,128]{2,1,0:T(8,128)}) custom-call(f32[1,32,128]{2,1,0:T(8,128)} %get-tuple-element.4.leaf_ref, f32[1,32,128]{2,1,0:T(8,128)} %get-tuple-element.5.inner_ref), custom_call_target="tpu_custom_call" | custom-call | tf_op jit(solution)/shard_map/write_out/pallas_call | solution.py:647

commit v2 on v1

--- a/solution.py
+++ b/solution.py
@@ -56,8 +56,8 @@
     leaf_upd_hbm,
     inner_inv_hbm,
     inner_upd_hbm,
-    leaf_hbm,
-    inner_hbm,
+    leaf_out,
+    inner_out,
     seeds_s,
     leaf_inv,
     leaf_upd,
@@ -85,8 +85,6 @@
     leaf_y,
     inner_y,
     leaf_v,
-    leaf_out,
-    inner_out,
     load_sem,
     small_sem,
     map_send,
@@ -103,7 +101,6 @@
     hop_x_recv,
     bulk_send,
     bulk_recv,
-    out_sem,
 ):
     x = lax.axis_index("leaf")
     m = lax.axis_index("front")
@@ -176,7 +173,8 @@
             device_id_type=MESH,
         )
 
-    bulk_rows = width // 4
+    pieces, early = 8, 3
+    bulk_rows = width // pieces
 
     def bulk_copy(piece, to):
         rows = pl.ds(piece * bulk_rows, bulk_rows)
@@ -241,8 +239,9 @@
     def _():
         for to in (0, 2, 3):
             map_to(to, 1).start()
-        bulk_copy(0, 0).start()
-        for q in range(4):
+        for q in range(early):
+            bulk_copy(q, 0).start()
+        for q in range(pieces):
             bulk_copy(q, 2).start()
 
     blocks = columns // BLOCK
@@ -423,7 +422,7 @@
 
         @pl.when(is_root)
         def _():
-            for q in range(1, 4):
+            for q in range(early, pieces):
                 bulk_copy(q, 0).start()
 
         def write_root_part(j, tile):
@@ -497,7 +496,7 @@
             own_chunk[SLOT_X, h] = result.astype(bf16)
             slot_x_copy(h, x + 1).start()
             share_start(SLOT_X, h, own_chunk.at[SLOT_X, h])
-            inner_out[rows_of(h)] = result
+            inner_out[0, rows_of(h)] = result
 
     @pl.when(jnp.logical_not(is_slot))
     def _():
@@ -505,7 +504,7 @@
             root_x_copy(h, x).wait_recv()
             own_chunk[ROOT_X, h] = hop_root_x[h].astype(bf16)
             share_start(ROOT_X, h, own_chunk.at[ROOT_X, h])
-            inner_out[rows_of(h)] = jnp.where(is_root, hop_root_x[h], 0.0)
+            inner_out[0, rows_of(h)] = jnp.where(is_root, hop_root_x[h], 0.0)
         for h in halves:
             x_root = share_finish(ROOT_X, h)
             leaf_v[rows_of(h)] = leaf_y[rows_of(h)] - rows_times(x_root, to_root)
@@ -517,15 +516,8 @@
         x_slot = share_finish(SLOT_X, h)
         s = (leaf_v[rows_of(h)] - rows_times(x_slot, to_slot)).astype(bf16)
         sum_start(LAST_SUM, h, s, leaf_inv)
-    inner_write = pltpu.make_async_copy(inner_out, inner_hbm.at[0], out_sem.at[2])
-    inner_write.start()
-    leaf_writes = [
-        pltpu.make_async_copy(leaf_out.at[rows_of(h)], leaf_hbm.at[0, rows_of(h)], out_sem.at[h])
-        for h in halves
-    ]
     for h in halves:
-        leaf_out[rows_of(h)] = sum_finish(LAST_SUM, h)
-        leaf_writes[h].start()
+        leaf_out[0, rows_of(h)] = sum_finish(LAST_SUM, h)
 
     for h in halves:
         for which in (LEAF_SUM, ROOT_SUM, LAST_SUM):
@@ -558,10 +550,6 @@
             map_to(to, 1).wait_send()
         for to in (0, 2):
             pltpu.make_async_copy(root_inv, root_inv, bulk_send.at[to // 2]).wait()
-
-    inner_write.wait()
-    for copy in leaf_writes:
-        copy.wait()
 
 
 def write_out(leaf_ref, inner_ref, leaf_hbm, inner_hbm, sem):
@@ -583,14 +571,21 @@
     rows = leaf_update.shape[2]
     f32, bf16 = jnp.float32, jnp.bfloat16
     dma = pltpu.SemaphoreType.DMA
+    vmem = pl.BlockSpec(memory_space=pltpu.VMEM)
     hbm = pl.BlockSpec(memory_space=pltpu.HBM)
     out = jax.ShapeDtypeStruct((1, probes, width), f32)
     part = (probes // 2, width)
+    operands = [
+        pltpu.with_memory_space_constraint(array, pltpu.HBM)
+        for array in (
+            probe_seeds, child_map, leaf_inverse, leaf_update, internal_inverse, internal_update,
+        )
+    ]
     leaf_part, inner_part = pl.pallas_call(
         functools.partial(kernel, fronts, probes, columns, width),
         out_shape=(out, out),
         in_specs=[hbm] * 6,
-        out_specs=(hbm, hbm),
+        out_specs=(vmem, vmem),
         scratch_shapes=[
             pltpu.SMEM((probes,), jnp.int32),
             pltpu.VMEM((width, columns), bf16),
@@ -619,8 +614,6 @@
             pltpu.VMEM((probes, width), f32),
             pltpu.VMEM((probes, width), f32),
             pltpu.VMEM((probes, width), f32),
-            pltpu.VMEM((probes, width), f32),
-            pltpu.VMEM((probes, width), f32),
             dma((4,)),
             dma((3,)),
             dma((leaves,)),
@@ -637,17 +630,16 @@
             dma((2, 2)),
             dma((2,)),
             dma,
-            dma((3,)),
         ],
         compiler_params=pltpu.CompilerParams(
-            collective_id=0, has_side_effects=True, vmem_limit_bytes=60 * 1024 * 1024
+            collective_id=0, has_side_effects=True, vmem_limit_bytes=48 * 1024 * 1024
         ),
         name="solves",
-    )(probe_seeds, child_map, leaf_inverse, leaf_update, internal_inverse, internal_update)
+    )(*operands)
     return pl.pallas_call(
         write_out,
         out_shape=(out, out),
-        in_specs=[hbm, hbm],
+        in_specs=[vmem, vmem],
         out_specs=(hbm, hbm),
         scratch_shapes=[dma((2,))],
         name="write_out",

time: 77.4 us -> 74.9 us (0.968)
  Pallas kernels: 76.7 us -> 72.9 us
  local copies, waits for them, and re-layouts: 0 us -> 1.19 us
    pallas_call x1, Pallas kernels: 74.6 us -> 71.5 us  [shards(): pl.pallas_call(functools.partial(kernel, fronts, probes, columns, width),...]
    unnamed x0 -> x4, local copies, waits for them, and re-layouts: none -> 1.19 us
where the time goes in v2:
time: 74.9 us; the launch traced here: 74.7 us
  Pallas kernels  72.9 us (97%)
  local copies, waits for them, and re-layouts  1.19 us (2%)
    pallas_call x1, Pallas kernels, shards(): pl.pallas_call(functools.partial(kernel, fronts, probes, columns, width),...  71.5 us

profile of v2, /device:TPU:3, one launch (start us, length us, event | category | flops | bytes accessed | tf_op | source)
XLA Modules:
  0.0 74.7 jit_solution(1158721537721031155)
XLA Ops:
  0.6 71.5 %solves.1 = (f32[1,32,128]{2,1,0:T(8,128)S(1)}, f32[1,32,128]{2,1,0:T(8,128)S(1)}) custom-call(s32[32]{0:T(128)} %seeds_hbm.1, s32[1,2,256]{2,1,0:T(2,128)} %maps_hbm.1, bf16[1,128,4096]{2,1,0:T(8,128)(2,1)} %leaf_inv_hbm.1, bf16[1,128,16384]{2,1,0:T(8,128)(2,1)} %leaf_upd_hbm.1, bf16[1,128,4096]{2,1,0:T(8,128)(2,1)} %inner_inv_hbm.1, ...), custom_call_target="tpu_custom_call" | custom-call | tf_op jit(solution)/shard_map/solves/pallas_call | solution.py:584
  72.1 0.0 copy-start
  72.2 0.6 copy-done
  72.7 0.0 copy-start.1
  72.7 0.6 copy-done.1
  73.3 1.4 %write_out.1 = (f32[1,32,128]{2,1,0:T(8,128)}, f32[1,32,128]{2,1,0:T(8,128)}) custom-call(f32[1,32,128]{2,1,0:T(8,128)} %copy-done, f32[1,32,128]{2,1,0:T(8,128)} %copy-done.1), custom_call_target="tpu_custom_call" | custom-call | tf_op jit(solution)/shard_map/write_out/pallas_call | solution.py:639
Async XLA Ops:
  72.1 0.6 copy-start
  72.7 0.6 copy-start.1

commit v3 on v2

v3 whole, which is shorter than its diff:
```python
import functools

import jax
import jax.numpy as jnp
from jax import lax
from jax.experimental import pallas as pl
from jax.experimental.pallas import tpu as pltpu
from jax.sharding import PartitionSpec as P

BLOCK = 64
MOD = 32749
MESH = pl.DeviceIdType.MESH
NT = (((1,), (1,)), ((), ()))
OFFSETS = (
    (2, 2), (2, 1), (1, 2), (2, 3), (3, 2), (2, 0), (0, 2), (1, 1),
    (3, 3), (1, 3), (3, 1), (1, 0), (0, 1), (3, 0), (0, 3), (0, 0),
)


def packed(values):
    word = sum(v << (2 * i) for i, v in enumerate(values))
    return word - (1 << 32) if word >= 1 << 31 else word


OFFSET_Z = packed([z for z, _ in OFFSETS])
OFFSET_Y = packed([y for _, y in OFFSETS])
CHIPS = 16
FAR_CHIPS = 5
FAR = 2 * FAR_CHIPS


def mod_prime(x):
    q = (x.astype(jnp.float32) * (1.0 / MOD)).astype(jnp.int32)
    r = x - q * MOD
    r = jnp.where(r < 0, r + MOD, r)
    return jnp.where(r >= MOD, r - MOD, r)


def probe_signs(seeds, node_id, columns, start, shape):
    index = node_id * columns + start + lax.broadcasted_iota(jnp.int32, shape, 1)
    wrapped = index >= MOD
    lower = jnp.where(wrapped, index - MOD, index)
    upper = jnp.where(wrapped, 1, 0)
    hashed = mod_prime(lower * 30011 + upper * 7717 + seeds)
    hashed = mod_prime(hashed * hashed)
    hashed = mod_prime(hashed * 21143 + lower)
    hashed = mod_prime(hashed * hashed + upper)
    return (1 - 2 * ((hashed >> 3) & 1)).astype(jnp.float32)


def kernel(
    fronts,
    probes,
    columns,
    width,
    seeds_hbm,
    maps_hbm,
    leaf_inv_hbm,
    leaf_upd_hbm,
    inner_inv_hbm,
    inner_upd_hbm,
    leaf_out,
    inner_out,
    seeds_s,
    leaf_inv,
    leaf_upd,
    inner_inv,
    inner_upd,
    to_slot,
    to_root,
    slot_root,
    signs,
    leaf_all,
    carried,
    all_maps,
    table_v,
    table_s,
    send_part,
    recv_part,
    recv_cross,
    own_chunk,
    recv_all,
    hop_send,
    hop_up,
    hop_root,
    leaf_y,
    inner_y,
    leaf_v,
    load_sem,
    small_sem,
    map_send,
    map_recv,
    part_send,
    part_recv,
    cross_send,
    cross_recv,
    all_send,
    all_recv,
    hop_up_send,
    hop_up_recv,
    hop_root_send,
    hop_root_recv,
    hop_x_send,
    hop_x_recv,
):
    x = lax.axis_index("leaf")
    m = lax.axis_index("front")
    m_z, m_y, m_c = m // 8, lax.rem(m // 2, 4), lax.rem(m, 2)
    leaves = 4
    f32, bf16 = jnp.float32, jnp.bfloat16
    is_slot = (x == 0) | (x == 2)
    is_root = x == 1
    part_rows = probes // 2
    halves = (0, 1)

    def rows_of(h):
        return pl.ds(h * part_rows, part_rows)

    seed_copy = pltpu.make_async_copy(seeds_hbm, seeds_s, small_sem.at[0])
    map_copy = pltpu.make_async_copy(maps_hbm.at[0], all_maps.at[x], small_sem.at[1])
    seed_copy.start()
    map_copy.start()
    loads = [
        pltpu.make_async_copy(src.at[0], dst, load_sem.at[i])
        for i, (src, dst) in enumerate(
            (
                (leaf_inv_hbm, leaf_inv),
                (leaf_upd_hbm, leaf_upd),
                (inner_upd_hbm, inner_upd),
                (inner_inv_hbm, inner_inv),
            )
        )
    ]
    loads[0].start()
    loads[1].start()

    def peer(i):
        at = i & 30
        z = (m_z + (jnp.int32(OFFSET_Z) >> at)) & 3
        y = (m_y + (jnp.int32(OFFSET_Y) >> at)) & 3
        return z * 8 + y * 2 + ((m_c + 1 + i) & 1)

    barrier = pltpu.get_barrier_semaphore()

    def greet_front(i, carry):
        pl.semaphore_signal(barrier, inc=1, device_id=(x, peer(i)), device_id_type=MESH)
        return carry

    lax.fori_loop(0, fronts - 1, greet_front, 0)
    for i in range(1, leaves):
        pl.semaphore_signal(
            barrier, inc=1, device_id=(lax.rem(x + i, leaves), m), device_id_type=MESH
        )

    def map_to(to, kind):
        return pltpu.make_async_remote_copy(
            src_ref=maps_hbm.at[0],
            dst_ref=all_maps.at[x],
            send_sem=map_send.at[to],
            recv_sem=map_recv.at[kind],
            device_id=(to, m),
            device_id_type=MESH,
        )

    def slot_map_copy(to):
        return pltpu.make_async_remote_copy(
            src_ref=maps_hbm.at[0],
            dst_ref=all_maps.at[x],
            send_sem=map_send.at[0],
            recv_sem=map_recv.at[0],
            device_id=(to, m),
            device_id_type=MESH,
        )

    greeted = fronts - 1 + leaves - 1

    @pl.when(is_slot)
    def _():
        pl.semaphore_wait(barrier, greeted)
        slot_map_copy(x + 1).start()

    seed_copy.wait()
    seeds = jnp.zeros((probes, 1), jnp.int32)
    row = lax.broadcasted_iota(jnp.int32, (probes, 1), 0)
    for p in range(probes):
        seeds = jnp.where(row == p, seeds_s[p], seeds)

    piece = 512

    def make_signs(i, carry):
        start = pl.multiple_of(i * piece, piece)
        z = probe_signs(seeds, x, columns, start, (probes, piece))
        signs[:, pl.ds(start, piece)] = z.astype(bf16)
        return carry

    lax.fori_loop(0, columns // piece, make_signs, 0)

    def rows_times(vector, matrix):
        return lax.dot_general(vector, matrix[...], NT, preferred_element_type=f32)

    loads[0].wait()
    leaf_y[...] = rows_times(signs[...], leaf_inv)
    yb_leaf = leaf_y[...].astype(bf16)
    loads[1].wait()
    loads[2].start()
    loads[3].start()
    wide = 2048

    def leaf_products(i, carry):
        at = pl.ds(pl.multiple_of(i * wide, wide), wide)
        leaf_all[:, at] = jnp.dot(
            yb_leaf, leaf_upd[:, at], preferred_element_type=f32
        ).astype(bf16)
        return carry

    lax.fori_loop(0, leaf_upd.shape[1] // wide, leaf_products, 0)
    map_copy.wait()

    @pl.when(jnp.logical_not(is_slot))
    def _():
        pl.semaphore_wait(barrier, greeted)

    @pl.when(is_root)
    def _():
        for to in (0, 2, 3):
            map_to(to, 1).start()

    blocks = columns // BLOCK
    count = all_maps.shape[2]
    target = lax.broadcasted_iota(jnp.int32, (blocks, count), 0)
    source = lax.broadcasted_iota(jnp.int32, (blocks, count), 1) + 1
    lane = lax.broadcasted_iota(jnp.int32, (blocks, 128), 1)
    sub = lax.broadcasted_iota(jnp.int32, (blocks, 128), 0)

    def find(values, wanted):
        return jnp.max(jnp.where(values == wanted, source, 0), axis=1, keepdims=True)

    def as_row(column):
        return jnp.sum(jnp.where(lane == sub, column, 0), axis=0, keepdims=True)

    def slot_map():
        pair = all_maps[pl.ds((x // 2) * 2, 1)][0]
        return jnp.where(x % 2 == 0, pair[0:1], pair[1:2])

    def table_out(which):
        copy = pltpu.make_async_copy(table_v.at[which], table_s.at[which], small_sem.at[2])
        copy.start()
        copy.wait()

    table_v[...] = jnp.zeros(table_v.shape, jnp.int32)

    @pl.when(jnp.logical_not(is_slot))
    def _():
        slot_map_copy(x).wait_recv()

    table_v[0, 0:1, :] = as_row(find(slot_map(), target))
    table_out(0)

    def pick(read, table, at, rows, order, write):
        left_half = lax.broadcasted_iota(jnp.int32, (rows, 128), 1) < BLOCK

        def half(entry, side):
            block = jnp.maximum(entry - 1, 0)
            odd = jnp.full((rows, 128), block & 1, jnp.int32)
            found = jnp.full((rows, 128), entry, jnp.int32)
            tile = read((block >> 1) * 128).astype(f32)
            turned = pltpu.roll(tile, BLOCK, 1)
            here = jnp.where(odd == side, tile, turned)
            return jnp.where(found > 0, here, 0.0)

        def body(i, carry):
            j = order(i)
            first = half(table_s[table, at, 2 * j], 0)
            second = half(table_s[table, at, 2 * j + 1], 1)
            write(i, jnp.where(left_half, first, second).astype(bf16))
            return carry

        lax.fori_loop(0, blocks // 2, body, 0, unroll=4)

    def pick_matrix(matrix, table, at, out):
        def write(j, tile):
            out[:, pl.ds(pl.multiple_of(j * 128, 128), 128)] = tile

        pick(lambda start: matrix[:, pl.ds(start, 128)], table, at, width, lambda j: j, write)

    def half_of(value, h):
        return value[h * part_rows : (h + 1) * part_rows]

    def pick_products(table, at, out):
        def write(i, tile):
            for h in halves:
                out[h, i] = half_of(tile, h)

        pick(lambda start: leaf_all[:, pl.ds(start, 128)], table, at, probes, peer, write)

    def send_each(low, high, to, src, dst, send_sem, recv_sem):
        def send(i, carry):
            pltpu.make_async_remote_copy(
                src_ref=src(i),
                dst_ref=dst(i),
                send_sem=send_sem,
                recv_sem=recv_sem,
                device_id=(to, peer(i)),
                device_id_type=MESH,
            ).start()
            return carry

        lax.fori_loop(low, high, send, 0, unroll=2)

    def wait_for(buffer, count, sem):
        part = buffer.at[pl.ds(0, count)]
        pltpu.make_async_copy(part, part, sem).wait()

    NEAR = fronts - 1 - FAR

    def send_far(which, h, cross=None, to=None):
        if cross is None:
            send_each(
                0, FAR, x,
                lambda i: send_part.at[which, h, i],
                lambda i: recv_part.at[which, h, i],
                part_send.at[which, h, 0], part_recv.at[which, h, 0],
            )
        else:
            send_each(
                0, FAR, to,
                lambda i: send_part.at[which, h, i],
                lambda i: recv_cross.at[cross, h, i],
                cross_send.at[0, h], cross_recv.at[cross, h],
            )

    def send_near(which, h):
        send_each(
            FAR, fronts - 1, x,
            lambda i: send_part.at[which, h, i],
            lambda i: recv_part.at[which, h, i],
            part_send.at[which, h, 1], part_recv.at[which, h, 1],
        )
        recv_part[which, h, fronts - 1] = send_part[which, h, fronts - 1]

    def columns_to(t):
        dz, dy = OFFSETS[t]
        chip = ((m_z + dz) & 3) * 4 + ((m_y + dy) & 3)
        return pl.ds(pl.multiple_of(chip * 256, 256), 256)

    def columns_from(t):
        dz, dy = OFFSETS[t]
        chip = ((m_z - dz) & 3) * 4 + ((m_y - dy) & 3)
        return pl.ds(pl.multiple_of(chip * 256, 256), 256)

    def sum_start(which, h, vector, matrix, more=None, cross=None, to=None):
        def chips(low, high):
            for t in range(low, high):
                partial = jnp.dot(vector, matrix[:, columns_to(t)], preferred_element_type=f32)
                for core in (0, 1):
                    i = 2 * t + (m_c if core else 1 - m_c)
                    chunk = partial[:, core * width : (core + 1) * width]
                    if more is not None:
                        chunk = chunk + more[h, i].astype(f32)
                    send_part[which, h, i] = chunk.astype(bf16)

        chips(0, FAR_CHIPS)
        send_far(which, h, cross, to)
        chips(FAR_CHIPS, CHIPS)
        send_near(which, h)

    def add_up(ref, low, high):
        sums = []
        for q in range(low, min(low + 4, high)):
            total = ref[q].astype(f32)
            for j in range(q + 4, high, 4):
                total = total + ref[j].astype(f32)
            sums.append(total)
        return (sums[0] + sums[1]) + (sums[2] + sums[3])

    def near_sum(which, h):
        wait_for(recv_part.at[which, h], NEAR, part_recv.at[which, h, 1])
        return add_up(recv_part.at[which, h], FAR, fronts)

    def sum_finish(which, h):
        total = near_sum(which, h)
        wait_for(recv_part.at[which, h], FAR, part_recv.at[which, h, 0])
        return total + add_up(recv_part.at[which, h], 0, FAR)

    def cross_sum(cross, h):
        wait_for(recv_cross.at[cross, h], FAR, cross_recv.at[cross, h])
        return add_up(recv_cross.at[cross, h], 0, FAR)

    own_at = fronts - 2 + m_c

    def share(which, h, chunk_ref, low, high, to, send_sem):
        send_each(
            low, high, to,
            lambda i: chunk_ref,
            lambda i: recv_all.at[which, h, (i & 30) + m_c],
            send_sem, all_recv.at[which, h, 0 if high == FAR else 1],
        )

    def share_far(which, h, chunk_ref):
        share(which, h, chunk_ref, 0, FAR, x, all_send.at[which, h, 0])

    def share_near(which, h, chunk_ref):
        share(which, h, chunk_ref, FAR, fronts - 1, x, all_send.at[which, h, 1])

    def share_cross(which, h, chunk_ref, to):
        share(which, h, chunk_ref, 0, FAR, to, cross_send.at[1, h])

    def share_all(which, h, chunk_ref):
        share_far(which, h, chunk_ref)
        share_near(which, h, chunk_ref)
        recv_all[which, h, own_at] = chunk_ref[...]

    def shared_times(which, h, matrix, waits=True):
        total = None
        for far, low, high in ((1, FAR_CHIPS, CHIPS), (0, 0, FAR_CHIPS)):
            if waits:
                wait_for(recv_all.at[which, h], NEAR if far else FAR, all_recv.at[which, h, far])
            for t in range(low, high):
                vector = jnp.concatenate(
                    [recv_all[which, h, 2 * t], recv_all[which, h, 2 * t + 1]], axis=1
                )
                term = rows_times(vector, matrix.at[:, columns_from(t)])
                total = term if total is None else total + term
        return total

    def hop(src, dst, send_sem, recv_sem, to):
        return pltpu.make_async_remote_copy(
            src_ref=src,
            dst_ref=dst,
            send_sem=send_sem,
            recv_sem=recv_sem,
            device_id=(to, m),
            device_id_type=MESH,
        )

    LEAF_SUM, ROOT_SUM, BACK_SUM, LAST_SUM = 0, 1, 2, 3
    RESIDUAL, ROOT_X, SLOT_X = 0, 1, 2

    def up_copy(h, to):
        return hop(hop_send.at[h], hop_up.at[h], hop_up_send.at[h], hop_up_recv.at[h], to)

    def root_copy(h, origin):
        return hop(
            hop_root.at[origin, h], hop_root.at[origin, h], hop_root_send.at[h], hop_root_recv.at[origin, h], 1
        )

    def root_x_copy(h, to):
        return hop(
            own_chunk.at[ROOT_X, h], recv_all.at[ROOT_X, h, own_at], hop_x_send.at[to, h], hop_x_recv.at[0, h], to
        )

    def slot_x_copy(h, to):
        return hop(
            own_chunk.at[SLOT_X, h], recv_all.at[SLOT_X, h, own_at], hop_x_send.at[0, h], hop_x_recv.at[1, h], to
        )

    pick_products(0, 0, send_part.at[LEAF_SUM])

    @pl.when(is_slot)
    def _():
        for h in halves:
            send_far(LEAF_SUM, h)
            send_near(LEAF_SUM, h)

    @pl.when(jnp.logical_not(is_slot))
    def _():
        for h in halves:
            send_far(LEAF_SUM, h, 0, x - 1)
            send_near(LEAF_SUM, h)

    @pl.when(jnp.logical_not(is_root))
    def _():
        map_to(0, 1).wait_recv()

    root_pair = all_maps[1]
    root_map = jnp.where(x // 2 == 0, root_pair[0:1], root_pair[1:2])
    inner = find(root_map, target)
    through = find(slot_map(), jnp.where(inner == 0, -1, inner + (blocks - 1)))
    table_v[1, 0:1, :] = as_row(through)
    table_v[1, 1:2, :] = as_row(inner)
    table_out(1)

    @pl.when(jnp.logical_not(is_slot))
    def _():
        for h in halves:
            hop_send[h] = near_sum(LEAF_SUM, h)
            up_copy(h, x - 1).start()
        pick_products(1, 0, send_part.at[ROOT_SUM])
        for h in halves:
            send_far(ROOT_SUM, h)
            send_near(ROOT_SUM, h)
        loads[2].wait()
        loads[3].wait()
        pick_matrix(leaf_upd, 0, 0, to_slot)
        pick_matrix(leaf_upd, 1, 0, to_root)

        @pl.when(x == 3)
        def _():
            for h in halves:
                hop_root[x, h] = sum_finish(ROOT_SUM, h)
                root_copy(h, x).start()

    @pl.when(is_slot)
    def _():
        pick_products(1, 0, carried)
        loads[2].wait()
        pick_matrix(inner_upd, 1, 1, slot_root)
        own_signs = probe_signs(seeds, x + 1 + leaves, columns, m * width, (probes, width))
        loads[3].wait()
        for h in halves:
            own_sum = sum_finish(LEAF_SUM, h)
            own_sum = own_sum + cross_sum(0, h)
            up_copy(h, x).wait_recv()
            own_chunk[RESIDUAL, h] = (half_of(own_signs, h) - (own_sum + hop_up[h])).astype(bf16)
            share_all(RESIDUAL, h, own_chunk.at[RESIDUAL, h])
        pick_matrix(leaf_upd, 0, 0, to_slot)
        for h in halves:
            y_slot = shared_times(RESIDUAL, h, inner_inv)
            inner_y[rows_of(h)] = y_slot
            sum_start(ROOT_SUM, h, y_slot.astype(bf16), slot_root, carried, x // 2, 1)
        pick_matrix(leaf_upd, 1, 0, to_root)
        for h in halves:
            hop_root[x, h] = near_sum(ROOT_SUM, h)
            root_copy(h, x).start()

    @pl.when(is_root)
    def _():
        own_signs = probe_signs(seeds, x + 1 + leaves, columns, m * width, (probes, width))
        for h in halves:
            total = sum_finish(ROOT_SUM, h)
            root_copy(h, 3).wait_recv()
            total = total + hop_root[3, h]
            for i in (0, 1):
                total = total + cross_sum(i, h)
            for i in (0, 1):
                root_copy(h, 2 * i).wait_recv()
                total = total + hop_root[2 * i, h]
            own_chunk[RESIDUAL, h] = (half_of(own_signs, h) - total).astype(bf16)
            share_all(RESIDUAL, h, own_chunk.at[RESIDUAL, h])
        for h in halves:
            y_root = shared_times(RESIDUAL, h, inner_inv)
            sum_start(BACK_SUM, h, y_root.astype(bf16), inner_inv)
        for h in halves:
            result = sum_finish(BACK_SUM, h)
            chunk = own_chunk.at[ROOT_X, h]
            chunk[...] = result.astype(bf16)
            for to in (0, 2):
                root_x_copy(h, to).start()
            for to in (0, 2):
                share_cross(ROOT_X, h, chunk, to)
            root_x_copy(h, 3).start()
            share_all(ROOT_X, h, chunk)
            inner_out[0, rows_of(h)] = result

    @pl.when(is_slot)
    def _():
        for h in halves:
            root_x_copy(h, 0).wait_recv()
            share_near(ROOT_X, h, recv_all.at[ROOT_X, h, own_at])

    @pl.when(x == 3)
    def _():
        for h in halves:
            root_x_copy(h, 0).wait_recv()
            share_far(ROOT_X, h, recv_all.at[ROOT_X, h, own_at])
            share_near(ROOT_X, h, recv_all.at[ROOT_X, h, own_at])
        inner_out[0] = jnp.zeros((probes, width), f32)

    @pl.when(is_slot)
    def _():
        for h in halves:
            v = shared_times(ROOT_X, h, slot_root)
            s = (inner_y[rows_of(h)] - v).astype(bf16)
            sum_start(BACK_SUM, h, s, inner_inv)
        for h in halves:
            leaf_v[rows_of(h)] = leaf_y[rows_of(h)] - shared_times(ROOT_X, h, to_root, False)
        for h in halves:
            result = sum_finish(BACK_SUM, h)
            chunk = own_chunk.at[SLOT_X, h]
            chunk[...] = result.astype(bf16)
            slot_x_copy(h, x + 1).start()
            share_cross(SLOT_X, h, chunk, x + 1)
            share_all(SLOT_X, h, chunk)
            inner_out[0, rows_of(h)] = result

    @pl.when(jnp.logical_not(is_slot))
    def _():
        for h in halves:
            leaf_v[rows_of(h)] = leaf_y[rows_of(h)] - shared_times(ROOT_X, h, to_root)
        for h in halves:
            slot_x_copy(h, x).wait_recv()
            share_near(SLOT_X, h, recv_all.at[SLOT_X, h, own_at])

    for h in halves:
        v = shared_times(SLOT_X, h, to_slot)
        s = (leaf_v[rows_of(h)] - v).astype(bf16)
        sum_start(LAST_SUM, h, s, leaf_inv)
    for h in halves:
        leaf_out[0, rows_of(h)] = sum_finish(LAST_SUM, h)

    def far_left(buffer, sem):
        wait_for(buffer, FAR, sem)

    def near_left(buffer, sem):
        wait_for(buffer, NEAR, sem)

    for h in halves:
        for which in (LEAF_SUM, ROOT_SUM, LAST_SUM):
            near_left(send_part.at[which, h], part_send.at[which, h, 1])
        far_left(send_part.at[LAST_SUM, h], part_send.at[LAST_SUM, h, 0])
        far_left(send_part.at[LEAF_SUM, h], cross_send.at[0, h])
        for which in (ROOT_X, SLOT_X):
            near_left(recv_all.at[which, h], all_send.at[which, h, 1])

    @pl.when(x != 3)
    def _():
        for h in halves:
            far_left(send_part.at[BACK_SUM, h], part_send.at[BACK_SUM, h, 0])
            near_left(send_part.at[BACK_SUM, h], part_send.at[BACK_SUM, h, 1])
            far_left(recv_all.at[RESIDUAL, h], all_send.at[RESIDUAL, h, 0])
            near_left(recv_all.at[RESIDUAL, h], all_send.at[RESIDUAL, h, 1])

    @pl.when(is_slot)
    def _():
        slot_map_copy(x + 1).wait_send()
        for h in halves:
            far_left(send_part.at[LEAF_SUM, h], part_send.at[LEAF_SUM, h, 0])
            root_copy(h, x).wait_send()
            far_left(recv_all.at[SLOT_X, h], all_send.at[SLOT_X, h, 0])
            far_left(recv_all.at[SLOT_X, h], cross_send.at[1, h])
            slot_x_copy(h, x + 1).wait_send()

    @pl.when(jnp.logical_not(is_slot))
    def _():
        for h in halves:
            up_copy(h, x - 1).wait_send()
            far_left(send_part.at[ROOT_SUM, h], part_send.at[ROOT_SUM, h, 0])
            far_left(recv_all.at[ROOT_X, h], all_send.at[ROOT_X, h, 0])

    @pl.when(x == 3)
    def _():
        for h in halves:
            root_copy(h, x).wait_send()

    @pl.when(is_root)
    def _():
        for to in (0, 2, 3):
            map_to(to, 1).wait_send()
        for h in halves:
            wait_for(recv_all.at[ROOT_X, h], 2 * FAR, cross_send.at[1, h])
            for to in (0, 2, 3):
                root_x_copy(h, to).wait_send()


def shards(probe_seeds, leaf_inverse, leaf_update, internal_inverse, internal_update, child_map):
    fronts = lax.axis_size("front")
    leaves = lax.axis_size("leaf")
    probes = probe_seeds.shape[0]
    width, columns = leaf_inverse.shape[1:]
    rows = leaf_update.shape[2]
    f32, bf16 = jnp.float32, jnp.bfloat16
    dma = pltpu.SemaphoreType.DMA
    vmem = pl.BlockSpec(memory_space=pltpu.VMEM)
    hbm = pl.BlockSpec(memory_space=pltpu.HBM)
    out = jax.ShapeDtypeStruct((1, probes, width), f32)
    part = (probes // 2, width)
    operands = [
        pltpu.with_memory_space_constraint(array, pltpu.HBM)
        for array in (
            probe_seeds, child_map, leaf_inverse, leaf_update, internal_inverse, internal_update,
        )
    ]
    return pl.pallas_call(
        functools.partial(kernel, fronts, probes, columns, width),
        out_shape=(out, out),
        in_specs=[hbm] * 6,
        out_specs=(vmem, vmem),
        scratch_shapes=[
            pltpu.SMEM((probes,), jnp.int32),
            pltpu.VMEM((width, columns), bf16),
            pltpu.VMEM((width, rows), bf16),
            pltpu.VMEM((width, columns), bf16),
            pltpu.VMEM((width, rows), bf16),
            pltpu.VMEM((width, columns), bf16),
            pltpu.VMEM((width, columns), bf16),
            pltpu.VMEM((width, columns), bf16),
            pltpu.VMEM((probes, columns), bf16),
            pltpu.VMEM((probes, rows), bf16),
            pltpu.VMEM((2, fronts, *part), bf16),
            pltpu.VMEM((leaves, *child_map.shape[1:]), jnp.int32),
            pltpu.VMEM((2, 8, 128), jnp.int32),
            pltpu.SMEM((2, 8, 128), jnp.int32),
            pltpu.VMEM((4, 2, fronts, *part), bf16),
            pltpu.VMEM((4, 2, fronts, *part), bf16),
            pltpu.VMEM((2, 2, FAR, *part), bf16),
            pltpu.VMEM((3, 2, *part), bf16),
            pltpu.VMEM((3, 2, fronts, *part), bf16),
            pltpu.VMEM((2, *part), f32),
            pltpu.VMEM((2, *part), f32),
            pltpu.VMEM((leaves, 2, *part), f32),
            pltpu.VMEM((probes, width), f32),
            pltpu.VMEM((probes, width), f32),
            pltpu.VMEM((probes, width), f32),
            dma((4,)),
            dma((3,)),
            dma((leaves,)),
            dma((2,)),
            dma((4, 2, 2)),
            dma((4, 2, 2)),
            dma((2, 2)),
            dma((2, 2)),
            dma((3, 2, 2)),
            dma((3, 2, 2)),
            dma((2,)),
            dma((2,)),
            dma((2,)),
            dma((leaves, 2)),
            dma((leaves, 2)),
            dma((2, 2)),
        ],
        compiler_params=pltpu.CompilerParams(
            collective_id=0, has_side_effects=True, vmem_limit_bytes=48 * 1024 * 1024
        ),
        name="solves",
    )(*operands)


def solution(mesh):
    return jax.shard_map(
        shards,
        mesh=mesh,
        in_specs=(
            P(),
            P("leaf", "front", None),
            P("leaf", "front", None),
            P("leaf", "front", None),
            P("leaf", "front", None),
            P("leaf", None, None),
        ),
        out_specs=(P("leaf", None, "front"), P("leaf", None, "front")),
        check_vma=False,
    )
```

time: 74.9 us -> 73.8 us (0.985)
  Pallas kernels: 72.9 us -> 71.9 us
    pallas_call x1 -> x0, Pallas kernels: 1.36 us -> none  [shards(): pl.pallas_call(write_out, out_shape=(out, out), in_specs=[vmem, vmem], ou...]
where the time goes in v3:
time: 73.8 us; the launch traced here: 73.7 us
  Pallas kernels  71.9 us (97%)
  local copies, waits for them, and re-layouts  1.21 us (2%)
    pallas_call x1, Pallas kernels, shards(): pl.pallas_call(functools.partial(kernel, fronts, probes, columns, width),...  71.9 us

profile of v3, /device:TPU:3, one launch (start us, length us, event | category | flops | bytes accessed | tf_op | source)
XLA Modules:
  0.0 73.7 jit_solution(7917676868391538860)
XLA Ops:
  0.6 71.9 %solves.1 = (f32[1,32,128]{2,1,0:T(8,128)S(1)}, f32[1,32,128]{2,1,0:T(8,128)S(1)}) custom-call(s32[32]{0:T(128)} %seeds_hbm.1, s32[1,2,256]{2,1,0:T(2,128)} %maps_hbm.1, bf16[1,128,4096]{2,1,0:T(8,128)(2,1)} %leaf_inv_hbm.1, bf16[1,128,16384]{2,1,0:T(8,128)(2,1)} %leaf_upd_hbm.1, bf16[1,128,4096]{2,1,0:T(8,128)(2,1)} %inner_inv_hbm.1, ...), custom_call_target="tpu_custom_call" | custom-call | tf_op jit(solution)/shard_map/solves/pallas_call | solution.py:673
  72.5 0.6 copy.10
  73.1 0.6 copy.11

commit v4 on v3

--- a/solution.py
+++ b/solution.py
@@ -27,6 +27,8 @@
 CHIPS = 16
 FAR_CHIPS = 5
 FAR = 2 * FAR_CHIPS
+TO_FIRST = (4, 8)
+TO_SECOND = 12
 
 
 def mod_prime(x):
@@ -69,11 +71,13 @@
     to_slot,
     to_root,
     slot_root,
+    root_inv,
     signs,
     leaf_all,
     carried,
     all_maps,
     table_v,
+    table_in,
     table_s,
     send_part,
     recv_part,
@@ -83,6 +87,7 @@
     hop_send,
     hop_up,
     hop_root,
+    hop_root_x,
     leaf_y,
     inner_y,
     leaf_v,
@@ -102,6 +107,8 @@
     hop_root_recv,
     hop_x_send,
     hop_x_recv,
+    bulk_send,
+    bulk_recv,
 ):
     x = lax.axis_index("leaf")
     m = lax.axis_index("front")
@@ -172,12 +179,21 @@
             device_id_type=MESH,
         )
 
+    pieces = 16
+    bulk_rows = width // pieces
+
+    def bulk_copy(piece, to):
+        rows = pl.ds(piece * bulk_rows, bulk_rows)
+        return pltpu.make_async_remote_copy(
+            src_ref=inner_inv_hbm.at[0, rows],
+            dst_ref=root_inv.at[rows],
+            send_sem=bulk_send.at[to // 2],
+            recv_sem=bulk_recv,
+            device_id=(to, m),
+            device_id_type=MESH,
+        )
+
     greeted = fronts - 1 + leaves - 1
-
-    @pl.when(is_slot)
-    def _():
-        pl.semaphore_wait(barrier, greeted)
-        slot_map_copy(x + 1).start()
 
     seed_copy.wait()
     seeds = jnp.zeros((probes, 1), jnp.int32)
@@ -204,6 +220,51 @@
     loads[1].wait()
     loads[2].start()
     loads[3].start()
+    blocks = columns // BLOCK
+    count = all_maps.shape[2]
+    target = lax.broadcasted_iota(jnp.int32, (blocks, count), 0)
+    source = lax.broadcasted_iota(jnp.int32, (blocks, count), 1) + 1
+    lane = lax.broadcasted_iota(jnp.int32, (blocks, 128), 1)
+    sub = lax.broadcasted_iota(jnp.int32, (blocks, 128), 0)
+
+    def find(values, wanted):
+        return jnp.max(jnp.where(values == wanted, source, 0), axis=1, keepdims=True)
+
+    def as_row(column):
+        return jnp.sum(jnp.where(lane == sub, column, 0), axis=0, keepdims=True)
+
+    def slot_map():
+        pair = all_maps[pl.ds((x // 2) * 2, 1)][0]
+        return jnp.where(x % 2 == 0, pair[0:1], pair[1:2])
+
+    def table_out(which):
+        copy = pltpu.make_async_copy(table_v.at[which], table_s.at[which], small_sem.at[2])
+        copy.start()
+        copy.wait()
+
+    table_v[...] = jnp.zeros(table_v.shape, jnp.int32)
+
+    def child_table_copy(to):
+        return pltpu.make_async_remote_copy(
+            src_ref=table_v.at[2],
+            dst_ref=table_in,
+            send_sem=map_send.at[1],
+            recv_sem=map_recv.at[2],
+            device_id=(to, m),
+            device_id_type=MESH,
+        )
+
+    @pl.when(is_slot)
+    def _():
+        map_copy.wait()
+        pair = all_maps[pl.ds(x, 1)][0]
+        table_v[0, 0:1, :] = as_row(find(pair[0:1], target))
+        table_v[2, 0:1, :] = as_row(find(pair[1:2], target))
+        pl.semaphore_wait(barrier, greeted)
+        child_table_copy(x + 1).start()
+        slot_map_copy(x + 1).start()
+        table_out(0)
+
     wide = 2048
 
     def leaf_products(i, carry):
@@ -214,47 +275,19 @@
         return carry
 
     lax.fori_loop(0, leaf_upd.shape[1] // wide, leaf_products, 0)
-    map_copy.wait()
-
     @pl.when(jnp.logical_not(is_slot))
     def _():
+        map_copy.wait()
         pl.semaphore_wait(barrier, greeted)
 
     @pl.when(is_root)
     def _():
         for to in (0, 2, 3):
             map_to(to, 1).start()
-
-    blocks = columns // BLOCK
-    count = all_maps.shape[2]
-    target = lax.broadcasted_iota(jnp.int32, (blocks, count), 0)
-    source = lax.broadcasted_iota(jnp.int32, (blocks, count), 1) + 1
-    lane = lax.broadcasted_iota(jnp.int32, (blocks, 128), 1)
-    sub = lax.broadcasted_iota(jnp.int32, (blocks, 128), 0)
-
-    def find(values, wanted):
-        return jnp.max(jnp.where(values == wanted, source, 0), axis=1, keepdims=True)
-
-    def as_row(column):
-        return jnp.sum(jnp.where(lane == sub, column, 0), axis=0, keepdims=True)
-
-    def slot_map():
-        pair = all_maps[pl.ds((x // 2) * 2, 1)][0]
-        return jnp.where(x % 2 == 0, pair[0:1], pair[1:2])
-
-    def table_out(which):
-        copy = pltpu.make_async_copy(table_v.at[which], table_s.at[which], small_sem.at[2])
-        copy.start()
-        copy.wait()
-
-    table_v[...] = jnp.zeros(table_v.shape, jnp.int32)
-
-    @pl.when(jnp.logical_not(is_slot))
-    def _():
-        slot_map_copy(x).wait_recv()
-
-    table_v[0, 0:1, :] = as_row(find(slot_map(), target))
-    table_out(0)
+        for q in range(TO_FIRST[0]):
+            bulk_copy(q, 0).start()
+        for q in range(TO_SECOND):
+            bulk_copy(q, 2).start()
 
     def pick(read, table, at, rows, order, write):
         left_half = lax.broadcasted_iota(jnp.int32, (rows, 128), 1) < BLOCK
@@ -313,8 +346,8 @@
 
     NEAR = fronts - 1 - FAR
 
-    def send_far(which, h, cross=None, to=None):
-        if cross is None:
+    def send_far(which, h, to=None):
+        if to is None:
             send_each(
                 0, FAR, x,
                 lambda i: send_part.at[which, h, i],
@@ -325,8 +358,8 @@
             send_each(
                 0, FAR, to,
                 lambda i: send_part.at[which, h, i],
-                lambda i: recv_cross.at[cross, h, i],
-                cross_send.at[0, h], cross_recv.at[cross, h],
+                lambda i: recv_cross.at[h, i],
+                cross_send.at[0, h], cross_recv.at[h],
             )
 
     def send_near(which, h):
@@ -348,7 +381,7 @@
         chip = ((m_z - dz) & 3) * 4 + ((m_y - dy) & 3)
         return pl.ds(pl.multiple_of(chip * 256, 256), 256)
 
-    def sum_start(which, h, vector, matrix, more=None, cross=None, to=None):
+    def sum_start(which, h, vector, matrix, more=None):
         def chips(low, high):
             for t in range(low, high):
                 partial = jnp.dot(vector, matrix[:, columns_to(t)], preferred_element_type=f32)
@@ -360,7 +393,7 @@
                     send_part[which, h, i] = chunk.astype(bf16)
 
         chips(0, FAR_CHIPS)
-        send_far(which, h, cross, to)
+        send_far(which, h)
         chips(FAR_CHIPS, CHIPS)
         send_near(which, h)
 
@@ -382,9 +415,9 @@
         wait_for(recv_part.at[which, h], FAR, part_recv.at[which, h, 0])
         return total + add_up(recv_part.at[which, h], 0, FAR)
 
-    def cross_sum(cross, h):
-        wait_for(recv_cross.at[cross, h], FAR, cross_recv.at[cross, h])
-        return add_up(recv_cross.at[cross, h], 0, FAR)
+    def cross_sum(h):
+        wait_for(recv_cross.at[h], FAR, cross_recv.at[h])
+        return add_up(recv_cross.at[h], 0, FAR)
 
     own_at = fronts - 2 + m_c
 
@@ -433,27 +466,32 @@
             device_id_type=MESH,
         )
 
-    LEAF_SUM, ROOT_SUM, BACK_SUM, LAST_SUM = 0, 1, 2, 3
-    RESIDUAL, ROOT_X, SLOT_X = 0, 1, 2
+    LEAF_SUM, ROOT_SUM, ROOT_BACK, SLOT_BACK, LAST_SUM = 0, 1, 2, 3, 4
+    SLOT_RHS, ROOT_RHS, ROOT_X, SLOT_X = 0, 1, 2, 3
 
     def up_copy(h, to):
-        return hop(hop_send.at[h], hop_up.at[h], hop_up_send.at[h], hop_up_recv.at[h], to)
-
-    def root_copy(h, origin):
+        return hop(hop_send.at[0, h], hop_up.at[h], hop_up_send.at[h], hop_up_recv.at[h], to)
+
+    def root_copy(h, i, origin, to):
         return hop(
-            hop_root.at[origin, h], hop_root.at[origin, h], hop_root_send.at[h], hop_root_recv.at[origin, h], 1
+            hop_root.at[origin, h], hop_root.at[origin, h], hop_root_send.at[i, h], hop_root_recv.at[origin, h], to
         )
 
     def root_x_copy(h, to):
-        return hop(
-            own_chunk.at[ROOT_X, h], recv_all.at[ROOT_X, h, own_at], hop_x_send.at[to, h], hop_x_recv.at[0, h], to
-        )
+        return hop(hop_send.at[1, h], hop_root_x.at[h], hop_x_send.at[1, h], hop_x_recv.at[0, h], to)
 
     def slot_x_copy(h, to):
         return hop(
             own_chunk.at[SLOT_X, h], recv_all.at[SLOT_X, h, own_at], hop_x_send.at[0, h], hop_x_recv.at[1, h], to
         )
 
+    @pl.when(jnp.logical_not(is_slot))
+    def _():
+        child_table_copy(x).wait_recv()
+        arrived = pltpu.make_async_copy(table_in, table_s.at[0], small_sem.at[2])
+        arrived.start()
+        arrived.wait()
+
     pick_products(0, 0, send_part.at[LEAF_SUM])
 
     @pl.when(is_slot)
@@ -465,12 +503,16 @@
     @pl.when(jnp.logical_not(is_slot))
     def _():
         for h in halves:
-            send_far(LEAF_SUM, h, 0, x - 1)
+            send_far(LEAF_SUM, h, x - 1)
             send_near(LEAF_SUM, h)
 
     @pl.when(jnp.logical_not(is_root))
     def _():
         map_to(0, 1).wait_recv()
+
+    @pl.when(jnp.logical_not(is_slot))
+    def _():
+        slot_map_copy(x).wait_recv()
 
     root_pair = all_maps[1]
     root_map = jnp.where(x // 2 == 0, root_pair[0:1], root_pair[1:2])
@@ -483,8 +525,14 @@
     @pl.when(jnp.logical_not(is_slot))
     def _():
         for h in halves:
-            hop_send[h] = near_sum(LEAF_SUM, h)
+            hop_send[0, h] = near_sum(LEAF_SUM, h)
             up_copy(h, x - 1).start()
+
+        @pl.when(is_root)
+        def _():
+            for q in range(*TO_FIRST):
+                bulk_copy(q, 0).start()
+
         pick_products(1, 0, send_part.at[ROOT_SUM])
         for h in halves:
             send_far(ROOT_SUM, h)
@@ -493,89 +541,66 @@
         loads[3].wait()
         pick_matrix(leaf_upd, 0, 0, to_slot)
         pick_matrix(leaf_upd, 1, 0, to_root)
-
-        @pl.when(x == 3)
+        for h in halves:
+            hop_root[x, h] = sum_finish(ROOT_SUM, h)
+            for i, to in enumerate((0, 2)):
+                root_copy(h, i, x, to).start()
+
+        @pl.when(is_root)
         def _():
-            for h in halves:
-                hop_root[x, h] = sum_finish(ROOT_SUM, h)
-                root_copy(h, x).start()
+            for q in range(TO_FIRST[1], pieces):
+                bulk_copy(q, 0).start()
+            for q in range(TO_SECOND, pieces):
+                bulk_copy(q, 2).start()
 
     @pl.when(is_slot)
     def _():
         pick_products(1, 0, carried)
         loads[2].wait()
         pick_matrix(inner_upd, 1, 1, slot_root)
-        own_signs = probe_signs(seeds, x + 1 + leaves, columns, m * width, (probes, width))
+        slot_signs = probe_signs(seeds, x + 1 + leaves, columns, m * width, (probes, width))
+        root_signs = probe_signs(seeds, 2 + leaves, columns, m * width, (probes, width))
         loads[3].wait()
         for h in halves:
             own_sum = sum_finish(LEAF_SUM, h)
-            own_sum = own_sum + cross_sum(0, h)
+            own_sum = own_sum + cross_sum(h)
             up_copy(h, x).wait_recv()
-            own_chunk[RESIDUAL, h] = (half_of(own_signs, h) - (own_sum + hop_up[h])).astype(bf16)
-            share_all(RESIDUAL, h, own_chunk.at[RESIDUAL, h])
+            own_chunk[SLOT_RHS, h] = (half_of(slot_signs, h) - (own_sum + hop_up[h])).astype(bf16)
+            share_all(SLOT_RHS, h, own_chunk.at[SLOT_RHS, h])
         pick_matrix(leaf_upd, 0, 0, to_slot)
         for h in halves:
-            y_slot = shared_times(RESIDUAL, h, inner_inv)
+            y_slot = shared_times(SLOT_RHS, h, inner_inv)
             inner_y[rows_of(h)] = y_slot
-            sum_start(ROOT_SUM, h, y_slot.astype(bf16), slot_root, carried, x // 2, 1)
+            sum_start(ROOT_SUM, h, y_slot.astype(bf16), slot_root, carried)
         pick_matrix(leaf_upd, 1, 0, to_root)
         for h in halves:
-            hop_root[x, h] = near_sum(ROOT_SUM, h)
-            root_copy(h, x).start()
-
-    @pl.when(is_root)
-    def _():
-        own_signs = probe_signs(seeds, x + 1 + leaves, columns, m * width, (probes, width))
-        for h in halves:
-            total = sum_finish(ROOT_SUM, h)
-            root_copy(h, 3).wait_recv()
-            total = total + hop_root[3, h]
-            for i in (0, 1):
-                total = total + cross_sum(i, h)
-            for i in (0, 1):
-                root_copy(h, 2 * i).wait_recv()
-                total = total + hop_root[2 * i, h]
-            own_chunk[RESIDUAL, h] = (half_of(own_signs, h) - total).astype(bf16)
-            share_all(RESIDUAL, h, own_chunk.at[RESIDUAL, h])
-        for h in halves:
-            y_root = shared_times(RESIDUAL, h, inner_inv)
-            sum_start(BACK_SUM, h, y_root.astype(bf16), inner_inv)
-        for h in halves:
-            result = sum_finish(BACK_SUM, h)
-            chunk = own_chunk.at[ROOT_X, h]
-            chunk[...] = result.astype(bf16)
-            for to in (0, 2):
-                root_x_copy(h, to).start()
-            for to in (0, 2):
-                share_cross(ROOT_X, h, chunk, to)
-            root_x_copy(h, 3).start()
-            share_all(ROOT_X, h, chunk)
-            inner_out[0, rows_of(h)] = result
-
-    @pl.when(is_slot)
-    def _():
-        for h in halves:
-            root_x_copy(h, 0).wait_recv()
-            share_near(ROOT_X, h, recv_all.at[ROOT_X, h, own_at])
-
-    @pl.when(x == 3)
-    def _():
-        for h in halves:
-            root_x_copy(h, 0).wait_recv()
-            share_far(ROOT_X, h, recv_all.at[ROOT_X, h, own_at])
-            share_near(ROOT_X, h, recv_all.at[ROOT_X, h, own_at])
-        inner_out[0] = jnp.zeros((probes, width), f32)
-
-    @pl.when(is_slot)
-    def _():
+            hop_root[x, h] = sum_finish(ROOT_SUM, h)
+            root_copy(h, 0, x, 2 - x).start()
+        for h in halves:
+            for origin in (1, 3):
+                root_copy(h, 0, origin, x).wait_recv()
+            root_copy(h, 0, 2 - x, x).wait_recv()
+            total = (hop_root[0, h] + hop_root[1, h]) + (hop_root[2, h] + hop_root[3, h])
+            own_chunk[ROOT_RHS, h] = (half_of(root_signs, h) - total).astype(bf16)
+            share_all(ROOT_RHS, h, own_chunk.at[ROOT_RHS, h])
+        pltpu.make_async_copy(root_inv, root_inv, bulk_recv).wait()
+        for h in halves:
+            y_root = shared_times(ROOT_RHS, h, root_inv)
+            sum_start(ROOT_BACK, h, y_root.astype(bf16), root_inv)
+        for h in halves:
+            result = sum_finish(ROOT_BACK, h)
+            own_chunk[ROOT_X, h] = result.astype(bf16)
+            share_all(ROOT_X, h, own_chunk.at[ROOT_X, h])
+            hop_send[1, h] = result
+            root_x_copy(h, x + 1).start()
         for h in halves:
             v = shared_times(ROOT_X, h, slot_root)
             s = (inner_y[rows_of(h)] - v).astype(bf16)
-            sum_start(BACK_SUM, h, s, inner_inv)
+            sum_start(SLOT_BACK, h, s, inner_inv)
         for h in halves:
             leaf_v[rows_of(h)] = leaf_y[rows_of(h)] - shared_times(ROOT_X, h, to_root, False)
         for h in halves:
-            result = sum_finish(BACK_SUM, h)
+            result = sum_finish(SLOT_BACK, h)
             chunk = own_chunk.at[SLOT_X, h]
             chunk[...] = result.astype(bf16)
             slot_x_copy(h, x + 1).start()
@@ -586,6 +611,11 @@
     @pl.when(jnp.logical_not(is_slot))
     def _():
         for h in halves:
+            root_x_copy(h, x).wait_recv()
+            own_chunk[ROOT_X, h] = hop_root_x[h].astype(bf16)
+            share_all(ROOT_X, h, own_chunk.at[ROOT_X, h])
+            inner_out[0, rows_of(h)] = jnp.where(is_root, hop_root_x[h], 0.0)
+        for h in halves:
             leaf_v[rows_of(h)] = leaf_y[rows_of(h)] - shared_times(ROOT_X, h, to_root)
         for h in halves:
             slot_x_copy(h, x).wait_recv()
@@ -607,25 +637,26 @@
     for h in halves:
         for which in (LEAF_SUM, ROOT_SUM, LAST_SUM):
             near_left(send_part.at[which, h], part_send.at[which, h, 1])
-        far_left(send_part.at[LAST_SUM, h], part_send.at[LAST_SUM, h, 0])
-        far_left(send_part.at[LEAF_SUM, h], cross_send.at[0, h])
+        for which in (ROOT_SUM, LAST_SUM):
+            far_left(send_part.at[which, h], part_send.at[which, h, 0])
+        far_left(recv_all.at[ROOT_X, h], all_send.at[ROOT_X, h, 0])
         for which in (ROOT_X, SLOT_X):
             near_left(recv_all.at[which, h], all_send.at[which, h, 1])
 
-    @pl.when(x != 3)
-    def _():
-        for h in halves:
-            far_left(send_part.at[BACK_SUM, h], part_send.at[BACK_SUM, h, 0])
-            near_left(send_part.at[BACK_SUM, h], part_send.at[BACK_SUM, h, 1])
-            far_left(recv_all.at[RESIDUAL, h], all_send.at[RESIDUAL, h, 0])
-            near_left(recv_all.at[RESIDUAL, h], all_send.at[RESIDUAL, h, 1])
-
     @pl.when(is_slot)
     def _():
         slot_map_copy(x + 1).wait_send()
+        child_table_copy(x + 1).wait_send()
         for h in halves:
             far_left(send_part.at[LEAF_SUM, h], part_send.at[LEAF_SUM, h, 0])
-            root_copy(h, x).wait_send()
+            for which in (ROOT_BACK, SLOT_BACK):
+                far_left(send_part.at[which, h], part_send.at[which, h, 0])
+                near_left(send_part.at[which, h], part_send.at[which, h, 1])
+            for which in (SLOT_RHS, ROOT_RHS):
+                far_left(recv_all.at[which, h], all_send.at[which, h, 0])
+                near_left(recv_all.at[which, h], all_send.at[which, h, 1])
+            root_copy(h, 0, x, 2 - x).wait_send()
+            root_x_copy(h, x + 1).wait_send()
             far_left(recv_all.at[SLOT_X, h], all_send.at[SLOT_X, h, 0])
             far_left(recv_all.at[SLOT_X, h], cross_send.at[1, h])
             slot_x_copy(h, x + 1).wait_send()
@@ -633,23 +664,17 @@
     @pl.when(jnp.logical_not(is_slot))
     def _():
         for h in halves:
+            far_left(send_part.at[LEAF_SUM, h], cross_send.at[0, h])
             up_copy(h, x - 1).wait_send()
-            far_left(send_part.at[ROOT_SUM, h], part_send.at[ROOT_SUM, h, 0])
-            far_left(recv_all.at[ROOT_X, h], all_send.at[ROOT_X, h, 0])
-
-    @pl.when(x == 3)
-    def _():
-        for h in halves:
-            root_copy(h, x).wait_send()
+            for i, to in enumerate((0, 2)):
+                root_copy(h, i, x, to).wait_send()
 
     @pl.when(is_root)
     def _():
         for to in (0, 2, 3):
             map_to(to, 1).wait_send()
-        for h in halves:
-            wait_for(recv_all.at[ROOT_X, h], 2 * FAR, cross_send.at[1, h])
-            for to in (0, 2, 3):
-                root_x_copy(h, to).wait_send()
+        for to in (0, 2):
+            pltpu.make_async_copy(root_inv, root_inv, bulk_send.at[to // 2]).wait()
 
 
 def shards(probe_seeds, leaf_inverse, leaf_update, internal_inverse, internal_update, child_map):
@@ -684,39 +709,44 @@
             pltpu.VMEM((width, columns), bf16),
             pltpu.VMEM((width, columns), bf16),
             pltpu.VMEM((width, columns), bf16),
+            pltpu.VMEM((width, columns), bf16),
             pltpu.VMEM((probes, columns), bf16),
             pltpu.VMEM((probes, rows), bf16),
             pltpu.VMEM((2, fronts, *part), bf16),
             pltpu.VMEM((leaves, *child_map.shape[1:]), jnp.int32),
-            pltpu.VMEM((2, 8, 128), jnp.int32),
+            pltpu.VMEM((3, 8, 128), jnp.int32),
+            pltpu.VMEM((8, 128), jnp.int32),
             pltpu.SMEM((2, 8, 128), jnp.int32),
+            pltpu.VMEM((5, 2, fronts, *part), bf16),
+            pltpu.VMEM((5, 2, fronts, *part), bf16),
+            pltpu.VMEM((2, FAR, *part), bf16),
+            pltpu.VMEM((4, 2, *part), bf16),
             pltpu.VMEM((4, 2, fronts, *part), bf16),
-            pltpu.VMEM((4, 2, fronts, *part), bf16),
-            pltpu.VMEM((2, 2, FAR, *part), bf16),
-            pltpu.VMEM((3, 2, *part), bf16),
-            pltpu.VMEM((3, 2, fronts, *part), bf16),
-            pltpu.VMEM((2, *part), f32),
+            pltpu.VMEM((2, 2, *part), f32),
             pltpu.VMEM((2, *part), f32),
             pltpu.VMEM((leaves, 2, *part), f32),
+            pltpu.VMEM((2, *part), f32),
             pltpu.VMEM((probes, width), f32),
             pltpu.VMEM((probes, width), f32),
             pltpu.VMEM((probes, width), f32),
             dma((4,)),
             dma((3,)),
             dma((leaves,)),
+            dma((3,)),
+            dma((5, 2, 2)),
+            dma((5, 2, 2)),
+            dma((2, 2)),
             dma((2,)),
             dma((4, 2, 2)),
             dma((4, 2, 2)),
+            dma((2,)),
+            dma((2,)),
+            dma((2, 2)),
+            dma((leaves, 2)),
             dma((2, 2)),
             dma((2, 2)),
-            dma((3, 2, 2)),
-            dma((3, 2, 2)),
             dma((2,)),
-            dma((2,)),
-            dma((2,)),
-            dma((leaves, 2)),
-            dma((leaves, 2)),
-            dma((2, 2)),
+            dma,
         ],
         compiler_params=pltpu.CompilerParams(
             collective_id=0, has_side_effects=True, vmem_limit_bytes=48 * 1024 * 1024

time: 73.8 us -> 72.2 us (0.978)
  Pallas kernels: 71.9 us -> 70.1 us
    pallas_call x1, Pallas kernels: 71.9 us -> 70.1 us  [shards(): pl.pallas_call(functools.partial(kernel, fronts, probes, columns, width),...]
where the time goes in v4:
time: 72.2 us; the launch traced here: 71.9 us
  Pallas kernels  70.1 us (97%)
  local copies, waits for them, and re-layouts  1.21 us (2%)
    pallas_call x1, Pallas kernels, shards(): pl.pallas_call(functools.partial(kernel, fronts, probes, columns, width),...  70.1 us

profile of v4, /device:TPU:3, one launch (start us, length us, event | category | flops | bytes accessed | tf_op | source)
XLA Modules:
  0.0 71.9 jit_solution(8304919241924464597)
XLA Ops:
  0.6 70.1 %solves.1 = (f32[1,32,128]{2,1,0:T(8,128)S(1)}, f32[1,32,128]{2,1,0:T(8,128)S(1)}) custom-call(s32[32]{0:T(128)} %seeds_hbm.1, s32[1,2,256]{2,1,0:T(2,128)} %maps_hbm.1, bf16[1,128,4096]{2,1,0:T(8,128)(2,1)} %leaf_inv_hbm.1, bf16[1,128,16384]{2,1,0:T(8,128)(2,1)} %leaf_upd_hbm.1, bf16[1,128,4096]{2,1,0:T(8,128)(2,1)} %inner_inv_hbm.1, ...), custom_call_target="tpu_custom_call" | custom-call | tf_op jit(solution)/shard_map/solves/pallas_call | solution.py:698
  70.7 0.6 copy.10
  71.3 0.6 copy.11

commit v5 on v4

--- a/solution.py
+++ b/solution.py
@@ -27,6 +27,7 @@
 CHIPS = 16
 FAR_CHIPS = 5
 FAR = 2 * FAR_CHIPS
+CROSS = 3
 TO_FIRST = (4, 8)
 TO_SECOND = 12
 
@@ -289,7 +290,7 @@
         for q in range(TO_SECOND):
             bulk_copy(q, 2).start()
 
-    def pick(read, table, at, rows, order, write):
+    def pick(read, table, at, rows, order, write, low=0, high=blocks // 2, unroll=4):
         left_half = lax.broadcasted_iota(jnp.int32, (rows, 128), 1) < BLOCK
 
         def half(entry, side):
@@ -308,7 +309,7 @@
             write(i, jnp.where(left_half, first, second).astype(bf16))
             return carry
 
-        lax.fori_loop(0, blocks // 2, body, 0, unroll=4)
+        lax.fori_loop(low, high, body, 0, unroll=unroll)
 
     def pick_matrix(matrix, table, at, out):
         def write(j, tile):
@@ -319,12 +320,12 @@
     def half_of(value, h):
         return value[h * part_rows : (h + 1) * part_rows]
 
-    def pick_products(table, at, out):
+    def pick_products(table, at, out, *part):
         def write(i, tile):
             for h in halves:
                 out[h, i] = half_of(tile, h)
 
-        pick(lambda start: leaf_all[:, pl.ds(start, 128)], table, at, probes, peer, write)
+        pick(lambda start: leaf_all[:, pl.ds(start, 128)], table, at, probes, peer, write, *part)
 
     def send_each(low, high, to, src, dst, send_sem, recv_sem):
         def send(i, carry):
@@ -410,10 +411,12 @@
         wait_for(recv_part.at[which, h], NEAR, part_recv.at[which, h, 1])
         return add_up(recv_part.at[which, h], FAR, fronts)
 
+    def far_sum(which, h):
+        wait_for(recv_part.at[which, h], FAR, part_recv.at[which, h, 0])
+        return add_up(recv_part.at[which, h], 0, FAR)
+
     def sum_finish(which, h):
-        total = near_sum(which, h)
-        wait_for(recv_part.at[which, h], FAR, part_recv.at[which, h, 0])
-        return total + add_up(recv_part.at[which, h], 0, FAR)
+        return near_sum(which, h) + far_sum(which, h)
 
     def cross_sum(h):
         wait_for(recv_cross.at[h], FAR, cross_recv.at[h])
@@ -492,19 +495,22 @@
         arrived.start()
         arrived.wait()
 
-    pick_products(0, 0, send_part.at[LEAF_SUM])
-
-    @pl.when(is_slot)
-    def _():
-        for h in halves:
+    pick_products(0, 0, send_part.at[LEAF_SUM], 0, FAR, 5)
+
+    def leaf_far(h):
+        @pl.when(x != CROSS)
+        def _():
             send_far(LEAF_SUM, h)
-            send_near(LEAF_SUM, h)
-
-    @pl.when(jnp.logical_not(is_slot))
-    def _():
-        for h in halves:
+
+        @pl.when(x == CROSS)
+        def _():
             send_far(LEAF_SUM, h, x - 1)
-            send_near(LEAF_SUM, h)
+
+    leaf_far(0)
+    pick_products(0, 0, send_part.at[LEAF_SUM], FAR, fronts, 11)
+    send_near(LEAF_SUM, 0)
+    leaf_far(1)
+    send_near(LEAF_SUM, 1)
 
     @pl.when(jnp.logical_not(is_root))
     def _():
@@ -526,6 +532,11 @@
     def _():
         for h in halves:
             hop_send[0, h] = near_sum(LEAF_SUM, h)
+
+            @pl.when(x != CROSS)
+            def _():
+                hop_send[0, h] = hop_send[0, h] + far_sum(LEAF_SUM, h)
+
             up_copy(h, x - 1).start()
 
         @pl.when(is_root)
@@ -563,8 +574,12 @@
         loads[3].wait()
         for h in halves:
             own_sum = sum_finish(LEAF_SUM, h)
-            own_sum = own_sum + cross_sum(h)
             up_copy(h, x).wait_recv()
+
+            @pl.when(x == CROSS - 1)
+            def _():
+                hop_up[h] = hop_up[h] + cross_sum(h)
+
             own_chunk[SLOT_RHS, h] = (half_of(slot_signs, h) - (own_sum + hop_up[h])).astype(bf16)
             share_all(SLOT_RHS, h, own_chunk.at[SLOT_RHS, h])
         pick_matrix(leaf_upd, 0, 0, to_slot)
@@ -648,7 +663,6 @@
         slot_map_copy(x + 1).wait_send()
         child_table_copy(x + 1).wait_send()
         for h in halves:
-            far_left(send_part.at[LEAF_SUM, h], part_send.at[LEAF_SUM, h, 0])
             for which in (ROOT_BACK, SLOT_BACK):
                 far_left(send_part.at[which, h], part_send.at[which, h, 0])
                 near_left(send_part.at[which, h], part_send.at[which, h, 1])
@@ -664,10 +678,19 @@
     @pl.when(jnp.logical_not(is_slot))
     def _():
         for h in halves:
-            far_left(send_part.at[LEAF_SUM, h], cross_send.at[0, h])
             up_copy(h, x - 1).wait_send()
             for i, to in enumerate((0, 2)):
                 root_copy(h, i, x, to).wait_send()
+
+    @pl.when(x == CROSS)
+    def _():
+        for h in halves:
+            far_left(send_part.at[LEAF_SUM, h], cross_send.at[0, h])
+
+    @pl.when(x != CROSS)
+    def _():
+        for h in halves:
+            far_left(send_part.at[LEAF_SUM, h], part_send.at[LEAF_SUM, h, 0])
 
     @pl.when(is_root)
     def _():

time: 72.2 us -> 72.1 us (level)
  no operation moved by 1% of the time
where the time goes in v5:
time: 72.1 us; the launch traced here: 72 us
  Pallas kernels  70.2 us (97%)
  local copies, waits for them, and re-layouts  1.21 us (2%)
    pallas_call x1, Pallas kernels, shards(): pl.pallas_call(functools.partial(kernel, fronts, probes, columns, width),...  70.2 us

profile of v5, /device:TPU:3, one launch (start us, length us, event | category | flops | bytes accessed | tf_op | source)
XLA Modules:
  0.0 72.0 jit_solution(12142641855045292026)
XLA Ops:
  0.6 70.2 %solves.1 = (f32[1,32,128]{2,1,0:T(8,128)S(1)}, f32[1,32,128]{2,1,0:T(8,128)S(1)}) custom-call(s32[32]{0:T(128)} %seeds_hbm.1, s32[1,2,256]{2,1,0:T(2,128)} %maps_hbm.1, bf16[1,128,4096]{2,1,0:T(8,128)(2,1)} %leaf_inv_hbm.1, bf16[1,128,16384]{2,1,0:T(8,128)(2,1)} %leaf_upd_hbm.1, bf16[1,128,4096]{2,1,0:T(8,128)(2,1)} %inner_inv_hbm.1, ...), custom_call_target="tpu_custom_call" | custom-call | tf_op jit(solution)/shard_map/solves/pallas_call | solution.py:721
  70.8 0.6 copy.10
  71.4 0.6 copy.11

commit v6 on v5

--- a/solution.py
+++ b/solution.py
@@ -275,7 +275,7 @@
         ).astype(bf16)
         return carry
 
-    lax.fori_loop(0, leaf_upd.shape[1] // wide, leaf_products, 0)
+    lax.fori_loop(0, leaf_upd.shape[1] // wide, leaf_products, 0, unroll=4)
     @pl.when(jnp.logical_not(is_slot))
     def _():
         map_copy.wait()

time: 72.1 us -> 72.1 us (level)
  no operation moved by 1% of the time
where the time goes in v6:
time: 72.1 us; the launch traced here: 72 us
  Pallas kernels  70.2 us (97%)
  local copies, waits for them, and re-layouts  1.21 us (2%)
    pallas_call x1, Pallas kernels, shards(): pl.pallas_call(functools.partial(kernel, fronts, probes, columns, width),...  70.2 us

profile of v6, /device:TPU:3, one launch (start us, length us, event | category | flops | bytes accessed | tf_op | source)
XLA Modules:
  0.0 72.0 jit_solution(16272055317852487799)
XLA Ops:
  0.6 70.2 %solves.1 = (f32[1,32,128]{2,1,0:T(8,128)S(1)}, f32[1,32,128]{2,1,0:T(8,128)S(1)}) custom-call(s32[32]{0:T(128)} %seeds_hbm.1, s32[1,2,256]{2,1,0:T(2,128)} %maps_hbm.1, bf16[1,128,4096]{2,1,0:T(8,128)(2,1)} %leaf_inv_hbm.1, bf16[1,128,16384]{2,1,0:T(8,128)(2,1)} %leaf_upd_hbm.1, bf16[1,128,4096]{2,1,0:T(8,128)(2,1)} %inner_inv_hbm.1, ...), custom_call_target="tpu_custom_call" | custom-call | tf_op jit(solution)/shard_map/solves/pallas_call | solution.py:721
  70.8 0.6 copy.10
  71.4 0.6 copy.11
